TPU v7x, 128 devices: a whole 4x4x4 slice. The times are simulated.
128 devices in a mesh: row: 4 (over x), col: 4 (over y), ka: 8 (over z, core).
Axes of the slice: x: 4, y: 4, z: 4, core: 2. Of those that a mesh axis runs over, the one named last changes fastest.
Arguments:
- amplitudes: float32 [5120, 32768], P(('row', 'col', 'ka')), may hold values from -6 to 6
- ladder: float32 [8, 2048, 32768], P(None, 'row', ('col', 'ka')), may hold values from -0.03125 to 0.03125
- pair_energy: float32 [5120], P(('col', 'ka')), may hold values from -3 to -0.5
- vir_energy: float32 [8, 2048], P(None, 'row'), may hold values from 0.5 to 4
- occ_count: int32 [8], replicated, may hold values from 1 to 1024, 5120 in all
- vir_count: int32 [8], replicated, may hold values from 1 to 32768, 163840 in all
Outputs:
- update: float32 [5120, 2048], P(('col', 'ka'), 'row')
Inputs may be any that keep to these rules, and one draw needn't show every extreme that they name: `occ_count`: each irrep holds at least one pair; the counts of all 8 irreps sum to 5120, and one irrep holds 1024. `vir_count`: the counts of all 8 irreps sum to 163840, and one irrep fills all 32768 slots.
All inputs are finite; a program needn't handle non-finite values.
Results may differ from a plain program's by a relative error of at most 0.0001.
Values sent between devices are 32-bit elements; how exact they have to be, the bound alone decides.
No kernel may reach another device: no remote copies, remote signals or barrier semaphores. Data moves between devices by JAX's collectives and lax.ppermute only.
A program may use at most 192 MiB of HBM per device.

v0:
```python
import jax
import jax.numpy as jnp
from jax import lax
from jax.sharding import PartitionSpec as P

OCC = 1024


def body(amplitudes, ladder, pair_energy, vir_energy, occ_count, vir_count):
    groups = ladder.shape[0]
    cd_local = ladder.shape[2]
    device_pos = lax.axis_index(("col", "ka"))
    cd_index = device_pos * cd_local + jnp.arange(cd_local, dtype=jnp.int32)
    cd_mask = (cd_index[None, :] < vir_count[:, None]).astype(jnp.float32)
    masked = ladder * cd_mask[:, None, :]
    ends = jnp.cumsum(occ_count)
    starts = ends - occ_count
    spread = lax.all_to_all(amplitudes, ("col", "ka"), split_axis=1, concat_axis=0, tiled=True)
    gathered = lax.all_gather(spread, "row", axis=0, tiled=True)
    total_rows = gathered.shape[0]
    positions = jnp.arange(total_rows, dtype=jnp.int32)
    irrep = jnp.sum((positions[:, None] >= ends[None, :]).astype(jnp.int32), axis=1)
    ab_local = ladder.shape[1]

    def add_group(group, partial_sums):
        first = jnp.minimum(starts[group], total_rows - OCC)
        window = lax.dynamic_slice_in_dim(gathered, first, OCC, 0)
        weights = lax.dynamic_index_in_dim(masked, group, 0, keepdims=False)
        product = jnp.dot(
            window, weights.T, precision=lax.Precision.HIGHEST, preferred_element_type=jnp.float32
        )
        chosen = lax.dynamic_slice_in_dim(irrep, first, OCC, 0) == group
        current = lax.dynamic_slice_in_dim(partial_sums, first, OCC, 0)
        current = current + jnp.where(chosen[:, None], product, jnp.float32(0.0))
        return lax.dynamic_update_slice_in_dim(partial_sums, current, first, 0)

    partial_sums = lax.fori_loop(
        0, groups, add_group, jnp.zeros((total_rows, ab_local), jnp.float32)
    )
    share = lax.psum_scatter(partial_sums, ("col", "ka"), scatter_dimension=0, tiled=True)
    rows_local = share.shape[0]
    row_index = device_pos * rows_local + jnp.arange(rows_local, dtype=jnp.int32)
    row_irrep = jnp.sum((row_index[:, None] >= ends[None, :]).astype(jnp.int32), axis=1)
    onehot = row_irrep[:, None] == jnp.arange(groups, dtype=jnp.int32)[None, :]
    vir_rows = jnp.sum(
        jnp.where(onehot[:, :, None], vir_energy[None, :, :], jnp.float32(0.0)), axis=1
    )
    count_rows = jnp.sum(jnp.where(onehot, vir_count[None, :], 0), axis=1)
    ab_index = lax.axis_index("row") * ab_local + jnp.arange(ab_local, dtype=jnp.int32)
    vir_mask = ab_index[None, :] < count_rows[:, None]
    denom = vir_rows - pair_energy[:, None]
    return jnp.where(vir_mask, share / denom, jnp.float32(0.0))


def solution(mesh):
    placed = (
        P(("row", "col", "ka"), None),
        P(None, "row", ("col", "ka")),
        P(("col", "ka")),
        P(None, "row"),
        P(),
        P(),
    )
    return jax.shard_map(
        body, mesh=mesh, in_specs=placed, out_specs=P(("col", "ka"), "row"), check_vma=False
    )
```

profile of v0, /device:TPU:0, one launch (start us, length us, event | category | flops | bytes accessed | tf_op | source)
XLA Modules:
  0.0 522.3 jit_solution(17848379504909399325)
XLA Ops:
  6.5 3.1 copy.12
  9.7 70.1 %all_to_all.19 = f32[40,32,1024]{2,0,1:T(8,128)} all-to-all(f32[40,32,1024]{2,0,1:T(8,128)S(1)} %bitcast.21), channel_id=1, replica_groups=mesh['row'=4,'col'=4,'ka'=8] {'col','ka'}, dimensions={1} | all-to-all | bytes 10485760 | tf_op jit(solution)/shard_map/all_to_all | solution.py:18
  79.9 0.2 reduce-window.8
  80.0 0.1 convert_reduce_fusion
  80.2 0.1 compare_convert_fusion
  80.3 13.3 %broadcast_multiply_fusion = f32[8,512,1024]{2,1,0:T(8,128)} fusion(f32[8,512,1024]{2,1,0:T(8,128)} %param.9, f32[8,1024]{1,0:T(8,128)S(1)} %compare_convert_fusion), kind=kLoop, calls=%fused_computation.7 | loop fusion | flops 4194304 | bytes 33587200 | tf_op jit(solution)/shard_map/mul | solution.py:15
  93.5 174.0 %all-gather.2.cloned.1.call-done = f32[5120,1024]{1,0:T(8,128)} async-done(((f32[1280,1024]{1,0:T(8,128)}), f32[5120,1024]{1,0:T(8,128)}) %all-gather.2.cloned.1.call-update) | async-done | bytes 20971536 | tf_op jit(solution)/shard_map/all_gather | solution.py:19
  267.6 5.3 %broadcast_in_dim.83 = f32[5120,512]{1,0:T(8,128)} broadcast(f32[]{:T(128)} %constant.71.clone.1), dimensions={} | broadcast | bytes 10485764 | tf_op jit(solution)/shard_map/broadcast_in_dim | solution.py:38
  272.9 142.0 %while.13 = (s32[]{:T(128)}, f32[5120,512]{1,0:T(8,128)}, s32[8]{0:T(128)S(1)}, s32[5120]{0:T(1024)S(1)}, f32[5120,1024]{1,0:T(8,128)}, /*index=5*/f32[8,512,102...) while((s32[]{:T(128)}, f32[5120,512]{1,0:T(8,128)}, s32[8]{0:T(128)S(1)}, s32[5120]{0:T(1024)S(1)}, ...), condition=%wide.region_5.6_spmd, body=%wide.region_4.5_spmd.sunk | while | flops 6443500544 | bytes 14687915 | solution.py:37
  272.9 0.6 dynamic_slice.57
  274.2 0.1 dynamic-slice_compare_fusion.2
  274.3 9.9 %select_add_fusion.2 = f32[1024,512]{1,0:T(8,128)S(1)} fusion(f32[5120,512]{1,0:T(8,128)} %get-tuple-element.175, s32[]{:T(128)S(6)} %select_n.47, pred[1024]{0:T(1024)(128)(4,1)S(1)} %dynamic-slice_compare_fusion.2, f32[8,512,1024]{2,1,0:T(8,128)} %get-tuple-element.189, s32[]{:T(128)} %get-tuple-element.174, f32[5120,1024]{1,0:T(8,128)} %get-tuple-element.188), kind=kOutput, calls=%fused_computation.3.clone.1 | convolution fusion | flops 6443499520 | bytes 10488320 | tf_op jit(solution)/shard_map/while/body/eval_jaxpr/dot_general | solution.py:29
  284.2 6.5 %dynamic_update_slice.8 = f32[5120,512]{1,0:T(8,128)} dynamic-update-slice(f32[5120,512]{1,0:T(8,128)} %get-tuple-element.175, f32[1024,512]{1,0:T(8,128)S(1)} %select_add_fusion.2, s32[]{:T(128)S(6)} %select_n.47, s32[]{:T(128)} %constant.70.clone.1..sunk) | dynamic-update-slice | bytes 4194308 | tf_op jit(solution)/shard_map/while/body/eval_jaxpr/dynamic_update_slice | solution.py:35
  290.7 0.6 dynamic_slice.57
  292.0 0.1 dynamic-slice_compare_fusion.2
  292.1 9.9 %select_add_fusion.2 = f32[1024,512]{1,0:T(8,128)S(1)} fusion(f32[5120,512]{1,0:T(8,128)} %get-tuple-element.175, s32[]{:T(128)S(6)} %select_n.47, pred[1024]{0:T(1024)(128)(4,1)S(1)} %dynamic-slice_compare_fusion.2, f32[8,512,1024]{2,1,0:T(8,128)} %get-tuple-element.189, s32[]{:T(128)} %get-tuple-element.174, f32[5120,1024]{1,0:T(8,128)} %get-tuple-element.188), kind=kOutput, calls=%fused_computation.3.clone.1 | convolution fusion | flops 6443499520 | bytes 10488320 | tf_op jit(solution)/shard_map/while/body/eval_jaxpr/dot_general | solution.py:29
  302.0 6.5 %dynamic_update_slice.8 = f32[5120,512]{1,0:T(8,128)} dynamic-update-slice(f32[5120,512]{1,0:T(8,128)} %get-tuple-element.175, f32[1024,512]{1,0:T(8,128)S(1)} %select_add_fusion.2, s32[]{:T(128)S(6)} %select_n.47, s32[]{:T(128)} %constant.70.clone.1..sunk) | dynamic-update-slice | bytes 4194308 | tf_op jit(solution)/shard_map/while/body/eval_jaxpr/dynamic_update_slice | solution.py:35
  308.5 0.6 dynamic_slice.57
  309.9 0.1 dynamic-slice_compare_fusion.2
  310.0 9.9 %select_add_fusion.2 = f32[1024,512]{1,0:T(8,128)S(1)} fusion(f32[5120,512]{1,0:T(8,128)} %get-tuple-element.175, s32[]{:T(128)S(6)} %select_n.47, pred[1024]{0:T(1024)(128)(4,1)S(1)} %dynamic-slice_compare_fusion.2, f32[8,512,1024]{2,1,0:T(8,128)} %get-tuple-element.189, s32[]{:T(128)} %get-tuple-element.174, f32[5120,1024]{1,0:T(8,128)} %get-tuple-element.188), kind=kOutput, calls=%fused_computation.3.clone.1 | convolution fusion | flops 6443499520 | bytes 10488320 | tf_op jit(solution)/shard_map/while/body/eval_jaxpr/dot_general | solution.py:29
  319.9 6.5 %dynamic_update_slice.8 = f32[5120,512]{1,0:T(8,128)} dynamic-update-slice(f32[5120,512]{1,0:T(8,128)} %get-tuple-element.175, f32[1024,512]{1,0:T(8,128)S(1)} %select_add_fusion.2, s32[]{:T(128)S(6)} %select_n.47, s32[]{:T(128)} %constant.70.clone.1..sunk) | dynamic-update-slice | bytes 4194308 | tf_op jit(solution)/shard_map/while/body/eval_jaxpr/dynamic_update_slice | solution.py:35
  326.4 0.6 dynamic_slice.57
  327.7 0.1 dynamic-slice_compare_fusion.2
  327.8 9.9 %select_add_fusion.2 = f32[1024,512]{1,0:T(8,128)S(1)} fusion(f32[5120,512]{1,0:T(8,128)} %get-tuple-element.175, s32[]{:T(128)S(6)} %select_n.47, pred[1024]{0:T(1024)(128)(4,1)S(1)} %dynamic-slice_compare_fusion.2, f32[8,512,1024]{2,1,0:T(8,128)} %get-tuple-element.189, s32[]{:T(128)} %get-tuple-element.174, f32[5120,1024]{1,0:T(8,128)} %get-tuple-element.188), kind=kOutput, calls=%fused_computation.3.clone.1 | convolution fusion | flops 6443499520 | bytes 10488320 | tf_op jit(solution)/shard_map/while/body/eval_jaxpr/dot_general | solution.py:29
  337.7 6.5 %dynamic_update_slice.8 = f32[5120,512]{1,0:T(8,128)} dynamic-update-slice(f32[5120,512]{1,0:T(8,128)} %get-tuple-element.175, f32[1024,512]{1,0:T(8,128)S(1)} %select_add_fusion.2, s32[]{:T(128)S(6)} %select_n.47, s32[]{:T(128)} %constant.70.clone.1..sunk) | dynamic-update-slice | bytes 4194308 | tf_op jit(solution)/shard_map/while/body/eval_jaxpr/dynamic_update_slice | solution.py:35
  344.2 0.6 dynamic_slice.57
  345.5 0.1 dynamic-slice_compare_fusion.2
  345.6 9.9 %select_add_fusion.2 = f32[1024,512]{1,0:T(8,128)S(1)} fusion(f32[5120,512]{1,0:T(8,128)} %get-tuple-element.175, s32[]{:T(128)S(6)} %select_n.47, pred[1024]{0:T(1024)(128)(4,1)S(1)} %dynamic-slice_compare_fusion.2, f32[8,512,1024]{2,1,0:T(8,128)} %get-tuple-element.189, s32[]{:T(128)} %get-tuple-element.174, f32[5120,1024]{1,0:T(8,128)} %get-tuple-element.188), kind=kOutput, calls=%fused_computation.3.clone.1 | convolution fusion | flops 6443499520 | bytes 10488320 | tf_op jit(solution)/shard_map/while/body/eval_jaxpr/dot_general | solution.py:29
  355.5 6.5 %dynamic_update_slice.8 = f32[5120,512]{1,0:T(8,128)} dynamic-update-slice(f32[5120,512]{1,0:T(8,128)} %get-tuple-element.175, f32[1024,512]{1,0:T(8,128)S(1)} %select_add_fusion.2, s32[]{:T(128)S(6)} %select_n.47, s32[]{:T(128)} %constant.70.clone.1..sunk) | dynamic-update-slice | bytes 4194308 | tf_op jit(solution)/shard_map/while/body/eval_jaxpr/dynamic_update_slice | solution.py:35
  362.0 0.6 dynamic_slice.57
  363.3 0.1 dynamic-slice_compare_fusion.2
  363.4 9.9 %select_add_fusion.2 = f32[1024,512]{1,0:T(8,128)S(1)} fusion(f32[5120,512]{1,0:T(8,128)} %get-tuple-element.175, s32[]{:T(128)S(6)} %select_n.47, pred[1024]{0:T(1024)(128)(4,1)S(1)} %dynamic-slice_compare_fusion.2, f32[8,512,1024]{2,1,0:T(8,128)} %get-tuple-element.189, s32[]{:T(128)} %get-tuple-element.174, f32[5120,1024]{1,0:T(8,128)} %get-tuple-element.188), kind=kOutput, calls=%fused_computation.3.clone.1 | convolution fusion | flops 6443499520 | bytes 10488320 | tf_op jit(solution)/shard_map/while/body/eval_jaxpr/dot_general | solution.py:29
  373.3 6.5 %dynamic_update_slice.8 = f32[5120,512]{1,0:T(8,128)} dynamic-update-slice(f32[5120,512]{1,0:T(8,128)} %get-tuple-element.175, f32[1024,512]{1,0:T(8,128)S(1)} %select_add_fusion.2, s32[]{:T(128)S(6)} %select_n.47, s32[]{:T(128)} %constant.70.clone.1..sunk) | dynamic-update-slice | bytes 4194308 | tf_op jit(solution)/shard_map/while/body/eval_jaxpr/dynamic_update_slice | solution.py:35
  379.8 0.6 dynamic_slice.57
  381.1 0.1 dynamic-slice_compare_fusion.2
  381.2 9.9 %select_add_fusion.2 = f32[1024,512]{1,0:T(8,128)S(1)} fusion(f32[5120,512]{1,0:T(8,128)} %get-tuple-element.175, s32[]{:T(128)S(6)} %select_n.47, pred[1024]{0:T(1024)(128)(4,1)S(1)} %dynamic-slice_compare_fusion.2, f32[8,512,1024]{2,1,0:T(8,128)} %get-tuple-element.189, s32[]{:T(128)} %get-tuple-element.174, f32[5120,1024]{1,0:T(8,128)} %get-tuple-element.188), kind=kOutput, calls=%fused_computation.3.clone.1 | convolution fusion | flops 6443499520 | bytes 10488320 | tf_op jit(solution)/shard_map/while/body/eval_jaxpr/dot_general | solution.py:29
  391.1 6.5 %dynamic_update_slice.8 = f32[5120,512]{1,0:T(8,128)} dynamic-update-slice(f32[5120,512]{1,0:T(8,128)} %get-tuple-element.175, f32[1024,512]{1,0:T(8,128)S(1)} %select_add_fusion.2, s32[]{:T(128)S(6)} %select_n.47, s32[]{:T(128)} %constant.70.clone.1..sunk) | dynamic-update-slice | bytes 4194308 | tf_op jit(solution)/shard_map/while/body/eval_jaxpr/dynamic_update_slice | solution.py:35
  397.6 0.6 dynamic_slice.57
  399.0 0.1 dynamic-slice_compare_fusion.2
  399.0 9.9 %select_add_fusion.2 = f32[1024,512]{1,0:T(8,128)S(1)} fusion(f32[5120,512]{1,0:T(8,128)} %get-tuple-element.175, s32[]{:T(128)S(6)} %select_n.47, pred[1024]{0:T(1024)(128)(4,1)S(1)} %dynamic-slice_compare_fusion.2, f32[8,512,1024]{2,1,0:T(8,128)} %get-tuple-element.189, s32[]{:T(128)} %get-tuple-element.174, f32[5120,1024]{1,0:T(8,128)} %get-tuple-element.188), kind=kOutput, calls=%fused_computation.3.clone.1 | convolution fusion | flops 6443499520 | bytes 10488320 | tf_op jit(solution)/shard_map/while/body/eval_jaxpr/dot_general | solution.py:29
  409.0 5.9 %dynamic_update_slice.8 = f32[5120,512]{1,0:T(8,128)} dynamic-update-slice(f32[5120,512]{1,0:T(8,128)} %get-tuple-element.175, f32[1024,512]{1,0:T(8,128)S(1)} %select_add_fusion.2, s32[]{:T(128)S(6)} %select_n.47, s32[]{:T(128)} %constant.70.clone.1..sunk) | dynamic-update-slice | bytes 4194308 | tf_op jit(solution)/shard_map/while/body/eval_jaxpr/dynamic_update_slice | solution.py:35
  414.9 0.1 convert_reduce_fusion.1
  415.0 0.1 copy.9
  415.2 0.1 select_reduce_fusion.1
  415.2 0.3 copy-done
  415.6 0.8 select_reduce_fusion
  416.4 97.2 %reduce-scatter.2.cloned.1.call-done = f32[160,512]{1,0:T(8,128)} async-done(((f32[5120,512]{1,0:T(8,128)}), f32[160,512]{1,0:T(8,128)}) %reduce-scatter.2.cloned.1.call-update) | async-done | bytes 327696 | tf_op jit(solution)/shard_map/reduce_scatter | solution.py:40
  513.7 1.8 divide_select_fusion
  (16 shorter events, 0.1 us)
Async XLA Ops:
  6.5 261.0 %all-gather.2.cloned.1.call-start = ((), (), s32[]{:S(2)}) async-start(), calls=%async_computation.2 | async-start | bytes 26214400 | tf_op jit(solution)/shard_map/all_gather | solution.py:19
  9.7 70.2 %copy-start.3 = (s32[8]{0:T(128)S(1)}, s32[8]{0:T(128)}, u32[]{:S(2)}) copy-start(s32[8]{0:T(128)} %param.12) | copy-start | bytes 100
  9.7 70.5 %copy-start.1 = (s32[8]{0:T(128)S(1)}, s32[8]{0:T(128)}, u32[]{:S(2)}) copy-start(s32[8]{0:T(128)} %param.13) | copy-start | bytes 100
  79.8 433.9 %reduce-scatter.2.cloned.1.call-start = ((), (), s32[]{:S(2)}) async-start(), calls=%async_computation.3 | async-start | bytes 10813440 | tf_op jit(solution)/shard_map/reduce_scatter | solution.py:40
  414.9 0.7 copy-start
  414.9 98.8 %copy-start.2 = (f32[160]{0:T(256)S(1)}, f32[160]{0:T(256)}, u32[]{:S(2)}) copy-start(f32[160]{0:T(256)} %param.10) | copy-start | bytes 1924
Sparse Core Ops, SparseCore 0:
  79.9 187.6 all-gather.1
  415.0 98.5 reduce-scatter.1
where the time goes:
time: 523 us; the launch traced here: 522 us
  waiting for transfers between devices  271 us (52%)
  matrix products  79.3 us (15%)
  blocking collectives  70.1 us (13%)
  local copies, waits for them, and re-layouts  65.3 us (12%)
  other arithmetic  17.1 us (3%)
  between operations  13.5 us (3%)
  loops' own time  5.57 us (1%)
    all_gather x1, waiting for transfers between devices, body(): gathered = lax.all_gather(spread, 'row', axis=0, tiled=True)  174 us
    reduce_scatter x1, waiting for transfers between devices, body(): lax.psum_scatter(partial_sums, ('col', 'ka'), scatter_dimension=0, tiled=...  97.2 us
    dot_general x8, matrix products, add_group(): jnp.dot(window, weights.T, precision=lax.Precision.HIGHEST, preferred_ele...  79.3 us
    all_to_all x1, blocking collectives, body(): lax.all_to_all(amplitudes, ('col', 'ka'), split_axis=1, concat_axis=0, ti...  70.1 us
    dynamic_update_slice x8, local copies, waits for them, and re-layouts, add_group(): return lax.dynamic_update_slice_in_dim(partial_sums, current, first, 0)  51.2 us
    mul x1, other arithmetic, body(): masked = ladder * cd_mask[:, None, :]  13.3 us
  transfers between devices with their start and end apart: 2, of which 2 were waited for; matrix products, arithmetic and copies ran while one was open for 3% of the time, Pallas kernels for 0%

commit v1 on v0

v1 whole, which is shorter than its diff:
```python
import jax
import jax.numpy as jnp
from jax import lax
from jax.experimental import pallas as pl
from jax.experimental.pallas import tpu as pltpu
from jax.sharding import PartitionSpec as P

STEP = 8
TILE = 256


def split(value):
    high = value.astype(jnp.bfloat16)
    return high, (value - high.astype(jnp.float32)).astype(jnp.bfloat16)


def split_kernel(count_ref, ladder_ref, high_ref, low_ref):
    group = pl.program_id(0)
    value = ladder_ref[0]
    column = lax.broadcasted_iota(jnp.int32, value.shape, 1)
    value = jnp.where(column < count_ref[group], value, jnp.float32(0.0))
    high, low = split(value)
    high_ref[0] = high
    low_ref[0] = low


def split_ladder(ladder, counts):
    groups, rows, cols = ladder.shape
    spec = pl.BlockSpec((1, rows, cols), lambda g, c: (g, 0, 0))
    half = jax.ShapeDtypeStruct(ladder.shape, jnp.bfloat16)
    return pl.pallas_call(
        split_kernel,
        grid_spec=pltpu.PrefetchScalarGridSpec(
            num_scalar_prefetch=1, grid=(groups,), in_specs=[spec], out_specs=[spec, spec]
        ),
        out_shape=[half, half],
        compiler_params=pltpu.CompilerParams(vmem_limit_bytes=40 << 20),
        name="split_ladder",
    )(counts, ladder)


def product_kernel(tile_ref, group_ref, bound_ref, rows_ref, high_ref, low_ref, out_ref, rows_high, rows_low):
    visit = pl.program_id(0)
    tile = tile_ref[visit]
    low_row = bound_ref[visit] - tile * TILE
    high_row = bound_ref[visit + 1] - tile * TILE

    @pl.when((visit == 0) | (tile != tile_ref[jnp.maximum(visit - 1, 0)]))
    def _():
        high, low = split(rows_ref[...])
        rows_high[...] = high
        rows_low[...] = low

    @pl.when(high_row > low_row)
    def _():
        def times(a, b):
            return lax.dot_general(a, b, (((1,), (1,)), ((), ())), preferred_element_type=jnp.float32)

        high, low = rows_high[...], rows_low[...]
        weights = high_ref[0]
        product = times(low, weights) + times(high, low_ref[0]) + times(high, weights)
        row = lax.broadcasted_iota(jnp.int32, product.shape, 0)
        out_ref[...] = jnp.where((row >= low_row) & (row < high_row), product, out_ref[...])


def products(rows, high, low, tile, group, bound):
    count, cols = rows.shape
    groups, ab, _ = high.shape
    weights = pl.BlockSpec((1, ab, cols), lambda v, t, g, b: (g[v], 0, 0))
    return pl.pallas_call(
        product_kernel,
        grid_spec=pltpu.PrefetchScalarGridSpec(
            num_scalar_prefetch=3,
            grid=(tile.shape[0],),
            in_specs=[pl.BlockSpec((TILE, cols), lambda v, t, g, b: (t[v], 0)), weights, weights],
            out_specs=pl.BlockSpec((TILE, ab), lambda v, t, g, b: (t[v], 0)),
            scratch_shapes=[pltpu.VMEM((TILE, cols), jnp.bfloat16), pltpu.VMEM((TILE, cols), jnp.bfloat16)],
        ),
        out_shape=jax.ShapeDtypeStruct((count, ab), jnp.float32),
        compiler_params=pltpu.CompilerParams(vmem_limit_bytes=40 << 20),
        name="ladder_products",
    )(tile, group, bound, rows, high, low)


def visits(ends, block_rows, blocks, chunks):
    chunk = jnp.arange(chunks, dtype=jnp.int32)[:, None]
    whole, rest = ends // block_rows, ends % block_rows
    chunk_ends = STEP * whole[None, :] + jnp.clip(rest[None, :] - STEP * chunk, 0, STEP)
    total = STEP * blocks
    tiles = total // TILE
    starts = jnp.broadcast_to(jnp.arange(tiles, dtype=jnp.int32)[None, :] * TILE, (chunks, tiles))
    marks = jnp.concatenate([starts, chunk_ends[:, :-1]], axis=1)
    number = marks.shape[1]
    place = jnp.arange(number, dtype=jnp.int32)
    before = (marks[:, None, :] < marks[:, :, None]) | (
        (marks[:, None, :] == marks[:, :, None]) & (place[None, None, :] < place[None, :, None])
    )
    rank = jnp.sum(before.astype(jnp.int32), axis=2)
    bound = jnp.sum(jnp.where(rank[:, :, None] == place[None, None, :], marks[:, :, None], 0), axis=1)
    tile = jnp.minimum(bound // TILE, tiles - 1)
    group = jnp.sum((chunk_ends[:, None, :] <= bound[:, :, None]).astype(jnp.int32), axis=2)
    group = jnp.minimum(group, ends.shape[0] - 1)
    bound = jnp.concatenate([bound, jnp.full((chunks, 1), total, jnp.int32)], axis=1)
    return tile, group, bound


def body(amplitudes, ladder, pair_energy, vir_energy, occ_count, vir_count):
    groups, ab_local, cd_local = ladder.shape
    plane = lax.axis_size(("col", "ka"))
    device_pos = lax.axis_index(("col", "ka"))
    block_rows = amplitudes.shape[0]
    chunks = block_rows // STEP
    blocks = plane * lax.axis_size("row")
    order = jnp.arange(groups, dtype=jnp.int32)
    ends = jnp.sum(jnp.where(order[None, :] <= order[:, None], occ_count[None, :], 0), axis=1)
    tile, group, bound = visits(ends, block_rows, blocks, chunks)
    high, low = split_ladder(ladder, vir_count - device_pos * cd_local)

    shares = []
    for chunk in range(chunks):
        own = amplitudes[chunk * STEP : (chunk + 1) * STEP].reshape(STEP, plane, cd_local).transpose(1, 0, 2)
        spread = lax.all_to_all(own, ("col", "ka"), split_axis=0, concat_axis=0, tiled=True)
        rows = lax.all_gather(spread, "row", axis=0, tiled=True).reshape(blocks * STEP, cd_local)
        partial = products(rows, high, low, tile[chunk], group[chunk], bound[chunk])
        share = lax.psum_scatter(partial, ("col", "ka"), scatter_dimension=0, tiled=True)
        shares.append(share.reshape(-1, STEP, ab_local))
    share = jnp.stack(shares, axis=1).reshape(-1, ab_local)

    rows_local = share.shape[0]
    row_index = device_pos * rows_local + jnp.arange(rows_local, dtype=jnp.int32)
    row_irrep = jnp.sum((row_index[:, None] >= ends[None, :]).astype(jnp.int32), axis=1)
    onehot = row_irrep[:, None] == order[None, :]
    vir_rows = jnp.sum(jnp.where(onehot[:, :, None], vir_energy[None, :, :], jnp.float32(0.0)), axis=1)
    count_rows = jnp.sum(jnp.where(onehot, vir_count[None, :], 0), axis=1)
    ab_index = lax.axis_index("row") * ab_local + jnp.arange(ab_local, dtype=jnp.int32)
    vir_mask = ab_index[None, :] < count_rows[:, None]
    denom = vir_rows - pair_energy[:, None]
    return jnp.where(vir_mask, share / denom, jnp.float32(0.0))


def solution(mesh):
    placed = (
        P(("row", "col", "ka"), None),
        P(None, "row", ("col", "ka")),
        P(("col", "ka")),
        P(None, "row"),
        P(),
        P(),
    )
    return jax.shard_map(
        body, mesh=mesh, in_specs=placed, out_specs=P(("col", "ka"), "row"), check_vma=False
    )
```

time: 523 us -> 703 us (1.34)
  waiting for transfers between devices: 271 us -> 457 us
  Pallas kernels: 0 us -> 96.1 us
  matrix products: 79.3 us -> 0 us
  local copies, waits for them, and re-layouts: 65.3 us -> 22.4 us
  blocking collectives: 70.1 us -> 109 us
  other arithmetic: 17.1 us -> 2.63 us
    reduce_scatter x1 -> x5, waiting for transfers between devices: 97.2 us -> 387 us  [body(): lax.psum_scatter(partial, ('col', 'ka'), scatter_dimension=0, tiled=True)]
    all_gather x1 -> x5, waiting for transfers between devices: 174 us -> 70.3 us  [body(): lax.all_gather(spread, 'row', axis=0, tiled=True)]
    pallas_call x0 -> x6, Pallas kernels: none -> 96.1 us  [the longest x5 83.9 us: products(): pl.pallas_call(product_kernel, grid_spec=pltpu.PrefetchScalarGridSpec(num...]
    dot_general x8 -> x0, matrix products: 79.3 us -> none  [add_group(): jnp.dot(window, weights.T, precision=lax.Precision.HIGHEST, preferred_ele...]
    dynamic_update_slice x8 -> x0, local copies, waits for them, and re-layouts: 51.2 us -> none  [add_group(): return lax.dynamic_update_slice_in_dim(partial_sums, current, first, 0)]
    all_to_all x1 -> x5, blocking collectives: 70.1 us -> 109 us  [body(): lax.all_to_all(own, ('col', 'ka'), split_axis=0, concat_axis=0, tiled=True)]
    unnamed x8 -> x24, local copies, waits for them, and re-layouts: 0.36 us -> 17.6 us
    mul x1 -> x3, other arithmetic: 13.3 us -> 0.02 us  [the longest x1 0.02 us: visits(): STEP * whole[None, :] + jnp.clip(rest[None, :] - STEP * chunk, 0, STEP)]
  transfers between devices with their start and end apart: 2 -> 10, of which waited for: 2 -> 8; matrix products, arithmetic and copies ran while one was open for 3% -> 1% of each run, Pallas kernels for 0% -> 14%
where the time goes in v1:
time: 703 us; the launch traced here: 701 us
  waiting for transfers between devices  457 us (65%)
  blocking collectives  109 us (16%)
  Pallas kernels  96.1 us (14%)
  local copies, waits for them, and re-layouts  22.4 us (3%)
  between operations  13.7 us (2%)
    reduce_scatter x5, waiting for transfers between devices, body(): lax.psum_scatter(partial, ('col', 'ka'), scatter_dimension=0, tiled=True)  387 us
    all_to_all x5, blocking collectives, body(): lax.all_to_all(own, ('col', 'ka'), split_axis=0, concat_axis=0, tiled=True)  109 us
    pallas_call x5, Pallas kernels, products(): pl.pallas_call(product_kernel, grid_spec=pltpu.PrefetchScalarGridSpec(num...  83.9 us
    all_gather x5, waiting for transfers between devices, body(): lax.all_gather(spread, 'row', axis=0, tiled=True)  70.3 us
    unnamed x24, local copies, waits for them, and re-layouts  17.6 us
  transfers between devices with their start and end apart: 10, of which 8 were waited for; matrix products, arithmetic and copies ran while one was open for 1% of the time, Pallas kernels for 14%

profile of v1, /device:TPU:0, one launch (start us, length us, event | category | flops | bytes accessed | tf_op | source)
XLA Modules:
  0.0 701.2 jit_solution(422082422654513649)
XLA Ops:
  6.5 3.8 fusion.10
  10.3 25.1 %all_to_all.25 = f32[32,8,1024]{2,1,0:T(8,128)} all-to-all(f32[32,8,1024]{2,1,0:T(8,128)S(1)} %bitcast.74), channel_id=1, replica_groups=mesh['row'=4,'col'=4,'ka'=8] {'col','ka'}, dimensions={0} | all-to-all | bytes 2097152 | tf_op jit(solution)/shard_map/all_to_all | solution.py:122
  35.5 0.0 all-gather.8.cloned.1.call-start
  35.5 21.4 %all_to_all.26 = f32[32,8,1024]{2,1,0:T(8,128)} all-to-all(f32[32,8,1024]{2,1,0:T(8,128)} %bitcast.73), channel_id=1, replica_groups=mesh['row'=4,'col'=4,'ka'=8] {'col','ka'}, dimensions={0} | all-to-all | bytes 2097152 | tf_op jit(solution)/shard_map/all_to_all | solution.py:122
  57.0 0.0 all-gather.10.cloned.1.call-start
  57.0 20.7 %all_to_all.27 = f32[32,8,1024]{2,1,0:T(8,128)} all-to-all(f32[32,8,1024]{2,1,0:T(8,128)S(1)} %bitcast.72), channel_id=1, replica_groups=mesh['row'=4,'col'=4,'ka'=8] {'col','ka'}, dimensions={0} | all-to-all | bytes 2097152 | tf_op jit(solution)/shard_map/all_to_all | solution.py:122
  77.8 0.0 all-gather.12.cloned.1.call-start
  77.9 20.8 %all_to_all.28 = f32[32,8,1024]{2,1,0:T(8,128)} all-to-all(f32[32,8,1024]{2,1,0:T(8,128)S(1)} %bitcast.71), channel_id=1, replica_groups=mesh['row'=4,'col'=4,'ka'=8] {'col','ka'}, dimensions={0} | all-to-all | bytes 2097152 | tf_op jit(solution)/shard_map/all_to_all | solution.py:122
  98.7 0.0 all-gather.14.cloned.1.call-start
  98.7 20.8 %all_to_all.29 = f32[32,8,1024]{2,1,0:T(8,128)} all-to-all(f32[32,8,1024]{2,1,0:T(8,128)S(1)} %bitcast.70), channel_id=1, replica_groups=mesh['row'=4,'col'=4,'ka'=8] {'col','ka'}, dimensions={0} | all-to-all | bytes 2097152 | tf_op jit(solution)/shard_map/all_to_all | solution.py:122
  119.5 0.0 reduce-scatter.6.cloned.1.call-start
  119.6 12.1 %split_ladder.1 = (bf16[8,512,1024]{2,1,0:T(8,128)(2,1)S(1)}, bf16[8,512,1024]{2,1,0:T(8,128)(2,1)}) custom-call(s32[8]{0:T(128)S(1)} %broadcast_subtract_fusion.count_ref, f32[8,512,1024]{2,1,0:T(8,128)} %ladder_ref.1), custom_call_target="tpu_custom_call" | custom-call | tf_op jit(solution)/shard_map/split_ladder/pallas_call | solution.py:31
  131.8 3.2 copy-done
  135.0 0.1 select_reduce_fusion.3
  135.2 0.1 clamp_add_fusion
  135.2 0.1 pad_add_fusion
  135.3 0.3 convert_reduce_fusion
  135.6 0.1 select_reduce_fusion.1
  135.7 0.1 convert_reduce_fusion.1
  135.9 2.2 copy-done.5
  138.1 17.1 %ladder_products.5 = f32[1024,512]{1,0:T(8,128)} custom-call(s32[11]{0:T(128)S(1)} %get-tuple-element.31.tile_ref, s32[11]{0:T(128)S(1)} %get-tuple-element.23.group_ref, s32[12]{0:T(128)S(1)} %get-tuple-element.18.bound_ref, f32[1024,1024]{1,0:T(8,128)S(1)} %bitcast.69, bf16[8,512,1024]{2,1,0:T(8,128)(2,1)} %copy-done, ...), custom_call_target="tpu_custom_call" | custom-call | tf_op jit(solution)/shard_map/ladder_products/pallas_call | solution.py:70
  155.2 0.0 reduce-scatter.8.cloned.1.call-start
  155.3 2.2 copy-done.4
  157.5 16.9 %ladder_products.6 = f32[1024,512]{1,0:T(8,128)} custom-call(s32[11]{0:T(128)S(1)} %get-tuple-element.32.tile_ref, s32[11]{0:T(128)S(1)} %get-tuple-element.22.group_ref, s32[12]{0:T(128)S(1)} %get-tuple-element.15.bound_ref, f32[1024,1024]{1,0:T(8,128)S(1)} %bitcast.68, bf16[8,512,1024]{2,1,0:T(8,128)(2,1)} %copy-done, ...), custom_call_target="tpu_custom_call" | custom-call | tf_op jit(solution)/shard_map/ladder_products/pallas_call | solution.py:70
  174.5 8.0 %all-gather.10.cloned.1.call-done = f32[128,8,1024]{2,1,0:T(8,128)} async-done(((f32[32,8,1024]{2,1,0:T(8,128)}), f32[128,8,1024]{2,1,0:T(8,128)}) %all-gather.10.cloned.1.call-update) | async-done | bytes 4194320 | tf_op jit(solution)/shard_map/all_gather | solution.py:123
  182.6 2.2 copy-done.3
  184.7 17.0 %ladder_products.7 = f32[1024,512]{1,0:T(8,128)} custom-call(s32[11]{0:T(128)S(1)} %get-tuple-element.33.tile_ref, s32[11]{0:T(128)S(1)} %get-tuple-element.21.group_ref, s32[12]{0:T(128)S(1)} %get-tuple-element.16.bound_ref, f32[1024,1024]{1,0:T(8,128)S(1)} %bitcast.67, bf16[8,512,1024]{2,1,0:T(8,128)(2,1)} %copy-done, ...), custom_call_target="tpu_custom_call" | custom-call | tf_op jit(solution)/shard_map/ladder_products/pallas_call | solution.py:70
  201.9 30.8 %all-gather.12.cloned.1.call-done = f32[128,8,1024]{2,1,0:T(8,128)} async-done(((f32[32,8,1024]{2,1,0:T(8,128)}), f32[128,8,1024]{2,1,0:T(8,128)}) %all-gather.12.cloned.1.call-update) | async-done | bytes 4194320 | tf_op jit(solution)/shard_map/all_gather | solution.py:123
  232.7 2.2 copy-done.2
  234.9 16.5 %ladder_products.8 = f32[1024,512]{1,0:T(8,128)} custom-call(s32[11]{0:T(128)S(1)} %get-tuple-element.34.tile_ref, s32[11]{0:T(128)S(1)} %get-tuple-element.20.group_ref, s32[12]{0:T(128)S(1)} %get-tuple-element.17.bound_ref, f32[1024,1024]{1,0:T(8,128)S(1)} %bitcast.66, bf16[8,512,1024]{2,1,0:T(8,128)(2,1)} %copy-done, ...), custom_call_target="tpu_custom_call" | custom-call | tf_op jit(solution)/shard_map/ladder_products/pallas_call | solution.py:70
  251.4 31.4 %all-gather.14.cloned.1.call-done = f32[128,8,1024]{2,1,0:T(8,128)} async-done(((f32[32,8,1024]{2,1,0:T(8,128)}), f32[128,8,1024]{2,1,0:T(8,128)}) %all-gather.14.cloned.1.call-update) | async-done | bytes 4194320 | tf_op jit(solution)/shard_map/all_gather | solution.py:123
  282.8 2.2 copy-done.1
  285.0 16.3 %ladder_products.9 = f32[1024,512]{1,0:T(8,128)} custom-call(s32[11]{0:T(128)S(1)} %get-tuple-element.35.tile_ref, s32[11]{0:T(128)S(1)} %get-tuple-element.19.group_ref, s32[12]{0:T(128)S(1)} %get-tuple-element.14.bound_ref, f32[1024,1024]{1,0:T(8,128)S(1)} %bitcast.65, bf16[8,512,1024]{2,1,0:T(8,128)(2,1)} %copy-done, ...), custom_call_target="tpu_custom_call" | custom-call | tf_op jit(solution)/shard_map/ladder_products/pallas_call | solution.py:70
  301.4 0.1 convert_reduce_fusion.2
  301.5 0.1 copy.10
  301.6 0.1 select_reduce_fusion.2
  301.7 0.8 select_reduce_fusion
  302.6 63.0 %reduce-scatter.6.cloned.1.call-done = f32[32,512]{1,0:T(8,128)} async-done(((f32[1024,512]{1,0:T(8,128)}), f32[32,512]{1,0:T(8,128)}) %reduce-scatter.6.cloned.1.call-update) | async-done | bytes 65552 | tf_op jit(solution)/shard_map/reduce_scatter | solution.py:125
  365.6 0.8 bitcast_dynamic-update-slice_fusion.4
  366.4 80.9 %reduce-scatter.8.cloned.1.call-done = f32[32,512]{1,0:T(8,128)} async-done(((f32[1024,512]{1,0:T(8,128)}), f32[32,512]{1,0:T(8,128)}) %reduce-scatter.8.cloned.1.call-update) | async-done | bytes 65552 | tf_op jit(solution)/shard_map/reduce_scatter | solution.py:125
  447.3 0.8 bitcast_dynamic-update-slice_fusion.3
  448.2 80.9 %reduce-scatter.10.cloned.1.call-done = f32[32,512]{1,0:T(8,128)} async-done(((f32[1024,512]{1,0:T(8,128)}), f32[32,512]{1,0:T(8,128)}) %reduce-scatter.10.cloned.1.call-update) | async-done | bytes 65552 | tf_op jit(solution)/shard_map/reduce_scatter | solution.py:125
  529.1 0.8 bitcast_dynamic-update-slice_fusion.2
  530.0 81.0 %reduce-scatter.12.cloned.1.call-done = f32[32,512]{1,0:T(8,128)} async-done(((f32[1024,512]{1,0:T(8,128)}), f32[32,512]{1,0:T(8,128)}) %reduce-scatter.12.cloned.1.call-update) | async-done | bytes 65552 | tf_op jit(solution)/shard_map/reduce_scatter | solution.py:125
  611.0 0.8 bitcast_dynamic-update-slice_fusion.1
  611.8 80.8 %reduce-scatter.14.cloned.1.call-done = f32[32,512]{1,0:T(8,128)} async-done(((f32[1024,512]{1,0:T(8,128)}), f32[32,512]{1,0:T(8,128)}) %reduce-scatter.14.cloned.1.call-update) | async-done | bytes 65552 | tf_op jit(solution)/shard_map/reduce_scatter | solution.py:125
  692.6 0.8 bitcast_dynamic-update-slice_fusion
  693.5 0.9 fusion
  (44 shorter events, 0.5 us)
Async XLA Ops:
  6.5 129.3 %all-gather.6.cloned.1.call-start = ((), (), s32[]{:S(2)}) async-start(), calls=%async_computation.10 | async-start | bytes 5242880 | tf_op jit(solution)/shard_map/all_gather | solution.py:123
  35.5 119.8 %all-gather.8.cloned.1.call-start = ((), (), s32[]{:S(2)}) async-start(), calls=%async_computation.12 | async-start | bytes 5242880 | tf_op jit(solution)/shard_map/all_gather | solution.py:123
  57.0 125.6 %all-gather.10.cloned.1.call-start = ((), (), s32[]{:S(2)}) async-start(), calls=%async_computation.14 | async-start | bytes 5242880 | tf_op jit(solution)/shard_map/all_gather | solution.py:123
  77.8 41.8 %copy-start.8 = (s32[8]{0:T(128)S(1)}, s32[8]{0:T(128)}, u32[]{:S(2)}) copy-start(s32[8]{0:T(128)} %param.11) | copy-start | bytes 100
  77.8 154.9 %all-gather.12.cloned.1.call-start = ((), (), s32[]{:S(2)}) async-start(), calls=%async_computation.16 | async-start | bytes 5242880 | tf_op jit(solution)/shard_map/all_gather | solution.py:123
  98.7 184.2 %all-gather.14.cloned.1.call-start = ((), (), s32[]{:S(2)}) async-start(), calls=%async_computation.18 | async-start | bytes 5242880 | tf_op jit(solution)/shard_map/all_gather | solution.py:123
  119.5 246.1 %reduce-scatter.6.cloned.1.call-start = ((), (), s32[]{:S(2)}) async-start(), calls=%async_computation.11 | async-start | bytes 2162688 | tf_op jit(solution)/shard_map/reduce_scatter | solution.py:125
  119.6 15.4 %copy-start.9 = (s32[8]{0:T(128)S(1)}, s32[8]{0:T(128)}, u32[]{:S(2)}) copy-start(s32[8]{0:T(128)} %param.10) | copy-start | bytes 100
  131.8 3.2 copy-start
  135.9 2.2 copy-start.5
  155.2 292.1 %reduce-scatter.8.cloned.1.call-start = ((), (), s32[]{:S(2)}) async-start(), calls=%async_computation.13 | async-start | bytes 2162688 | tf_op jit(solution)/shard_map/reduce_scatter | solution.py:125
  155.3 2.2 copy-start.4
  174.5 354.6 %reduce-scatter.10.cloned.1.call-start = ((), (), s32[]{:S(2)}) async-start(), calls=%async_computation.15 | async-start | bytes 2162688 | tf_op jit(solution)/shard_map/reduce_scatter | solution.py:125
  182.6 2.2 copy-start.3
  201.8 409.1 %reduce-scatter.12.cloned.1.call-start = ((), (), s32[]{:S(2)}) async-start(), calls=%async_computation.17 | async-start | bytes 2162688 | tf_op jit(solution)/shard_map/reduce_scatter | solution.py:125
  232.7 2.2 copy-start.2
  251.4 441.2 %reduce-scatter.14.cloned.1.call-start = ((), (), s32[]{:S(2)}) async-start(), calls=%async_computation.19 | async-start | bytes 2162688 | tf_op jit(solution)/shard_map/reduce_scatter | solution.py:125
  282.8 2.2 copy-start.1
  285.0 16.7 %copy-start.6 = (f32[8,512]{1,0:T(8,128)S(1)}, f32[8,512]{1,0:T(8,128)}, u32[]{:S(2)}) copy-start(f32[8,512]{1,0:T(8,128)} %param.9) | copy-start | bytes 49156
  285.0 408.5 %copy-start.7 = (f32[160]{0:T(256)S(1)}, f32[160]{0:T(256)}, u32[]{:S(2)}) copy-start(f32[160]{0:T(256)} %param.8) | copy-start | bytes 1924
Sparse Core Ops, SparseCore 0:
  35.6 46.3 all-gather.5
  83.7 48.5 all-gather.7
  133.9 48.5 all-gather.9
  184.1 48.5 all-gather.11
  234.2 48.5 all-gather.13
  286.2 79.3 reduce-scatter.5
  369.1 78.1 reduce-scatter.7
  450.9 78.1 reduce-scatter.9
  532.7 78.2 reduce-scatter.11
  614.3 78.2 reduce-scatter.13

commit v2 on v1

v2 whole, which is shorter than its diff:
```python
import jax
import jax.numpy as jnp
from jax import lax
from jax.experimental import pallas as pl
from jax.experimental.pallas import tpu as pltpu
from jax.sharding import Mesh, PartitionSpec as P

STEP = 8
TILE = 128
CORES = 2


def split(value):
    high = value.astype(jnp.bfloat16)
    return high, (value - high.astype(jnp.float32)).astype(jnp.bfloat16)


def split_kernel(count_ref, ladder_ref, high_ref, low_ref):
    group = pl.program_id(0)
    value = ladder_ref[0]
    column = lax.broadcasted_iota(jnp.int32, value.shape, 1)
    value = jnp.where(column < count_ref[group], value, jnp.float32(0.0))
    high, low = split(value.T)
    high_ref[0] = high
    low_ref[0] = low


def split_ladder(ladder, counts):
    groups, rows, cols = ladder.shape
    spec = pl.BlockSpec((1, rows, cols), lambda g, c: (g, 0, 0))
    turned = pl.BlockSpec((1, cols, rows), lambda g, c: (g, 0, 0))
    half = jax.ShapeDtypeStruct((groups, cols, rows), jnp.bfloat16)
    return pl.pallas_call(
        split_kernel,
        grid_spec=pltpu.PrefetchScalarGridSpec(
            num_scalar_prefetch=1, grid=(groups,), in_specs=[spec], out_specs=[turned, turned]
        ),
        out_shape=[half, half],
        compiler_params=pltpu.CompilerParams(vmem_limit_bytes=40 << 20),
        cost_estimate=pl.CostEstimate(flops=8 * ladder.size, transcendentals=0, bytes_accessed=8 * ladder.size),
        name="split_ladder",
    )(counts, ladder)


def product_kernel(
    bound_ref, place_ref, own, left, right, far_a, far_b, high, low, mine, other,
    rows, weights_high, weights_low, out, row_sems, weight_sems, out_sems,
):
    groups = high.shape[0]
    plane_rows = own.shape[0]
    planes = rows.shape[0] // plane_rows
    total = rows.shape[0]
    x, core = place_ref[0], place_ref[1]

    def place(step, shift=0):
        return pl.multiple_of(lax.rem(x + step, planes) * plane_rows + shift, STEP)

    half = far_a.shape[0]
    row_copies = [
        pltpu.make_async_copy(source, rows.at[pl.ds(start, source.shape[0])], row_sems.at[i])
        for i, (source, start) in enumerate(
            [
                (own, place(0)),
                (left, place(planes - 1)),
                (right, place(1)),
                (far_a, place(2)),
                (far_b, place(2, half)),
            ]
        )
    ]
    for copy in row_copies:
        copy.start()
    weight_copies = []
    for group in range(groups):
        pair = (
            pltpu.make_async_copy(high.at[group], weights_high.at[group], weight_sems.at[0, group]),
            pltpu.make_async_copy(low.at[group], weights_low.at[group], weight_sems.at[1, group]),
        )
        for copy in pair:
            copy.start()
        weight_copies.append(pair)
    for copy in row_copies:
        copy.wait()

    def times(a, b):
        return lax.dot_general(a, b, (((1,), (0,)), ((), ())), preferred_element_type=jnp.float32)

    for group in range(groups):
        for copy in weight_copies[group]:
            copy.wait()
        first, last = bound_ref[group], bound_ref[group + 1]
        start = lax.div(first, STEP) * STEP
        number = jnp.where(last > first, lax.div(last - start + (TILE - 1), TILE), 0)

        def visit(step, carry, group=group, first=first, last=last, start=start):
            at = pl.multiple_of(jnp.minimum(start + step * TILE, total - TILE), STEP)
            a_high, a_low = split(rows[pl.ds(at, TILE), :])
            weights = weights_high[group]
            product = times(a_low, weights) + times(a_high, weights_low[group]) + times(a_high, weights)
            row = lax.broadcasted_iota(jnp.int32, product.shape, 0) + at
            kept = out[pl.ds(at, TILE), :]
            out[pl.ds(at, TILE), :] = jnp.where((row >= first) & (row < last), product, kept)
            return carry

        lax.fori_loop(0, number, visit, 0)

    pieces, piece_rows, _ = mine.shape
    out_copies = []
    for piece in range(pieces):
        base = piece * CORES * piece_rows
        for kind, (target, which) in enumerate([(other, 1 - core), (mine, core)]):
            start = pl.multiple_of(base + which * piece_rows, STEP)
            copy = pltpu.make_async_copy(
                out.at[pl.ds(start, piece_rows)], target.at[piece], out_sems.at[kind, piece]
            )
            copy.start()
            out_copies.append(copy)
    for copy in out_copies:
        copy.wait()


def products(bound, place, parts, high, low, pieces, piece_rows):
    groups, cols, ab = high.shape
    total = pieces * CORES * piece_rows
    hbm = pl.BlockSpec(memory_space=pltpu.HBM)
    smem = pl.BlockSpec(memory_space=pltpu.SMEM)
    half = jax.ShapeDtypeStruct((pieces, piece_rows, ab), jnp.float32)
    return pl.pallas_call(
        product_kernel,
        in_specs=[smem, smem] + [hbm] * (len(parts) + 2),
        out_specs=[hbm, hbm],
        out_shape=[half, half],
        scratch_shapes=[
            pltpu.VMEM((total, cols), jnp.float32),
            pltpu.VMEM((groups, cols, ab), jnp.bfloat16),
            pltpu.VMEM((groups, cols, ab), jnp.bfloat16),
            pltpu.VMEM((total, ab), jnp.float32),
            pltpu.SemaphoreType.DMA((len(parts),)),
            pltpu.SemaphoreType.DMA((2, groups)),
            pltpu.SemaphoreType.DMA((2, pieces)),
        ],
        compiler_params=pltpu.CompilerParams(vmem_limit_bytes=48 << 20),
        cost_estimate=pl.CostEstimate(
            flops=12 * total * ab * cols, transcendentals=0, bytes_accessed=4 * (groups * ab * cols + total * (ab + cols))
        ),
        name="ladder_products",
    )(bound, place, *parts, high, low)


def ring(size, step):
    return [(i, (i + step) % size) for i in range(size)]


def after(value, *others):
    return lax.optimization_barrier((value, others))[0]


def body(amplitudes, ladder, pair_energy, vir_energy, occ_count, vir_count):
    groups, ab_local, cd_local = ladder.shape
    rows_x, cols_y, depth = lax.axis_size("row"), lax.axis_size("col"), lax.axis_size("deep")
    plane = cols_y * depth * CORES
    x, core = lax.axis_index("row"), lax.axis_index("core")
    device_pos = lax.axis_index(("col", "deep", "core"))
    block_rows = amplitudes.shape[0]
    chunks = block_rows // STEP
    order = jnp.arange(groups, dtype=jnp.int32)
    ends = jnp.sum(jnp.where(order[None, :] <= order[:, None], occ_count[None, :], 0), axis=1)
    within = jnp.arange(chunks, dtype=jnp.int32)[:, None] * STEP
    bounds = STEP * (ends // block_rows)[None, :] + jnp.clip((ends % block_rows)[None, :] - within, 0, STEP)
    bounds = jnp.concatenate([jnp.zeros((chunks, 1), jnp.int32), bounds], axis=1)
    place = jnp.stack([x, core]).astype(jnp.int32)
    high, low = split_ladder(ladder, vir_count - device_pos * cd_local)

    spreads = []
    for chunk in range(chunks):
        rows = amplitudes
        if chunk:
            rows = after(rows, spreads[-1])
        own = rows[chunk * STEP : (chunk + 1) * STEP].reshape(STEP, plane, cd_local).transpose(1, 0, 2)
        spread = lax.all_to_all(own, ("col", "deep", "core"), split_axis=0, concat_axis=0, tiled=True)
        spreads.append(spread.reshape(plane * STEP, cd_local))

    def pair(left, right):
        return lax.ppermute(left, "row", ring(rows_x, 1)), lax.ppermute(right, "row", ring(rows_x, rows_x - 1))

    half = plane * STEP // 2
    near = [pair(spread, spread) for spread in spreads]
    far = [pair(left[:half], right[half:]) for left, right in near]

    parts, shares = [], []
    piece_rows = STEP * rows_x
    for chunk in range(chunks):
        ready = list(near[chunk + 1 : chunk + 2]) + spreads[chunk + 2 : chunk + 3] + parts[-2:-1] + shares[-3:-2]
        inputs = (spreads[chunk], *near[chunk], *far[chunk])
        inputs = after(inputs, *ready)
        mine, other = products(bounds[chunk], place, inputs, high, low, cols_y * depth, piece_rows)
        part = mine + lax.ppermute(other, "core", ring(CORES, 1))
        parts.append(part)
        met = lax.all_to_all(part, ("col", "deep"), split_axis=0, concat_axis=0, tiled=True)
        shares.append(jnp.sum(met, axis=0))
    share = jnp.stack([share.reshape(-1, STEP, ab_local) for share in shares], axis=1).reshape(-1, ab_local)

    rows_local = share.shape[0]
    row_index = device_pos * rows_local + jnp.arange(rows_local, dtype=jnp.int32)
    row_irrep = jnp.sum((row_index[:, None] >= ends[None, :]).astype(jnp.int32), axis=1)
    onehot = row_irrep[:, None] == order[None, :]
    vir_rows = jnp.sum(jnp.where(onehot[:, :, None], vir_energy[None, :, :], jnp.float32(0.0)), axis=1)
    count_rows = jnp.sum(jnp.where(onehot, vir_count[None, :], 0), axis=1)
    ab_index = x * ab_local + jnp.arange(ab_local, dtype=jnp.int32)
    vir_mask = ab_index[None, :] < count_rows[:, None]
    denom = vir_rows - pair_energy[:, None]
    return jnp.where(vir_mask, share / denom, jnp.float32(0.0))


def solution(mesh):
    shape = mesh.devices.shape
    mesh = Mesh(mesh.devices.reshape(shape[0], shape[1], -1, CORES), ("row", "col", "deep", "core"))
    plane = ("col", "deep", "core")
    placed = (
        P(("row", *plane), None),
        P(None, "row", plane),
        P(plane),
        P(None, "row"),
        P(),
        P(),
    )
    return jax.shard_map(
        body, mesh=mesh, in_specs=placed, out_specs=P(plane, "row"), check_vma=False
    )
```

time: 703 us -> 314 us (0.45)
  waiting for transfers between devices: 457 us -> 52.2 us
  starting transfers between devices: 0.38 us -> 85.4 us
  blocking collectives: 109 us -> 25 us
  other arithmetic: 2.63 us -> 18.3 us
  local copies, waits for them, and re-layouts: 22.4 us -> 37 us
  between operations: 13.7 us -> 0.45 us
    reduce_scatter x5 -> x0, waiting for transfers between devices: 387 us -> none  [body(): lax.psum_scatter(partial, ('col', 'ka'), scatter_dimension=0, tiled=True)]
    all_to_all x5 -> x1, blocking collectives: 109 us -> 25 us  [body(): lax.all_to_all(own, ('col', 'deep', 'core'), split_axis=0, concat_axis=0,...]
    all_gather x5 -> x0, waiting for transfers between devices: 70.3 us -> none  [body(): lax.all_gather(spread, 'row', axis=0, tiled=True)]
    all_to_all x0 -> x9, starting transfers between devices: none -> 52.3 us  [the longest x5 32 us: body(): lax.all_to_all(part, ('col', 'deep'), split_axis=0, concat_axis=0, tiled=...]
    all_to_all x0 -> x9, waiting for transfers between devices: none -> 49.5 us  [the longest x5 29.7 us: body(): lax.all_to_all(part, ('col', 'deep'), split_axis=0, concat_axis=0, tiled=...]
    ppermute x0 -> x25, starting transfers between devices: none -> 33.1 us  [the longest x10 27 us: pair(): lax.ppermute(right, 'row', ring(rows_x, rows_x - 1))]
    slice x1 -> x15, local copies, waits for them, and re-layouts: 3.81 us -> 30.2 us  [the longest x10 18.9 us: body(): far = [pair(left[:half], right[half:]) for left, right in near]]
    add x2 -> x7, other arithmetic: 0.08 us -> 12.2 us  [the longest x5 12.1 us: body(): part = mine + lax.ppermute(other, 'core', ring(CORES, 1))]
  transfers between devices with their start and end apart: 10 -> 34, of which waited for: 8 -> 6; matrix products, arithmetic and copies ran while one was open for 1% -> 14% of each run, Pallas kernels for 14% -> 30%
where the time goes in v2:
time: 314 us; the launch traced here: 312 us
  Pallas kernels  93.2 us (30%)
  starting transfers between devices  85.4 us (27%)
  waiting for transfers between devices  52.2 us (17%)
  local copies, waits for them, and re-layouts  37 us (12%)
  blocking collectives  25 us (8%)
  other arithmetic  18.3 us (6%)
    pallas_call x5, Pallas kernels, products(): pl.pallas_call(product_kernel, in_specs=[smem, smem] + [hbm] * (len(parts...  79.7 us
    all_to_all x5, starting transfers between devices, body(): lax.all_to_all(part, ('col', 'deep'), split_axis=0, concat_axis=0, tiled=...  32 us
    all_to_all x5, waiting for transfers between devices, body(): lax.all_to_all(part, ('col', 'deep'), split_axis=0, concat_axis=0, tiled=...  29.7 us
    ppermute x10, starting transfers between devices, pair(): lax.ppermute(right, 'row', ring(rows_x, rows_x - 1))  27 us
    all_to_all x1, blocking collectives, body(): lax.all_to_all(own, ('col', 'deep', 'core'), split_axis=0, concat_axis=0,...  25 us
    all_to_all x4, starting transfers between devices, body(): lax.all_to_all(own, ('col', 'deep', 'core'), split_axis=0, concat_axis=0,...  20.3 us
    all_to_all x4, waiting for transfers between devices, body(): lax.all_to_all(own, ('col', 'deep', 'core'), split_axis=0, concat_axis=0,...  19.8 us
    slice x10, local copies, waits for them, and re-layouts, body(): far = [pair(left[:half], right[half:]) for left, right in near]  18.9 us
  transfers between devices with their start and end apart: 34, of which 6 were waited for; matrix products, arithmetic and copies ran while one was open for 14% of the time, Pallas kernels for 30%

profile of v2, /device:TPU:0, one launch (start us, length us, event | category | flops | bytes accessed | tf_op | source)
XLA Modules:
  0.0 311.6 jit_solution(13717202015105017764)
XLA Ops:
  1.3 25.0 %all_to_all.50 = f32[32,8,1024]{2,1,0:T(8,128)S(1)} all-to-all(f32[32,8,1024]{2,1,0:T(8,128)S(1)} %bitcast.57), channel_id=1, replica_groups=mesh['row'=4,'col'=4,'deep'=4,'core'=2] {'col','deep','core'}, dimensions={0} | all-to-all | bytes 2097152 | tf_op jit(solution)/shard_map/all_to_all | solution.py:180
  26.3 2.7 slice.64
  29.0 4.1 %all-to-all-start.1 = ((f32[32,8,1024]{2,1,0:T(8,128)}), f32[32,8,1024]{2,1,0:T(8,128)S(1)}, u32[]{:S(2)}, u32[]{:S(2)}) async-start(f32[32,8,1024]{2,1,0:T(8,128)} %bitcast.7), calls=%async_computation.1 | async-start | bytes 2097152 | tf_op jit(solution)/shard_map/all_to_all | solution.py:180
  36.4 13.5 %all-to-all-done.1 = f32[32,8,1024]{2,1,0:T(8,128)S(1)} async-done(((f32[32,8,1024]{2,1,0:T(8,128)}), f32[32,8,1024]{2,1,0:T(8,128)S(1)}, u32[]{:S(2)}, u32[]{:S(2)}) %all-to-all-start.1) | async-done | bytes 1048608 | tf_op jit(solution)/shard_map/all_to_all | solution.py:180
  49.9 2.7 slice.65
  52.6 4.1 %all-to-all-start.2 = ((f32[32,8,1024]{2,1,0:T(8,128)}), f32[32,8,1024]{2,1,0:T(8,128)S(1)}, u32[]{:S(2)}, u32[]{:S(2)}) async-start(f32[32,8,1024]{2,1,0:T(8,128)} %bitcast.55), calls=%async_computation.2 | async-start | bytes 2097152 | tf_op jit(solution)/shard_map/all_to_all | solution.py:180
  60.1 1.9 slice.80
  62.3 1.9 slice.81
  64.2 3.0 collective-permute-start.3
  67.2 6.3 %all-to-all-done.2 = f32[32,8,1024]{2,1,0:T(8,128)S(1)} async-done(((f32[32,8,1024]{2,1,0:T(8,128)}), f32[32,8,1024]{2,1,0:T(8,128)S(1)}, u32[]{:S(2)}, u32[]{:S(2)}) %all-to-all-start.2) | async-done | bytes 1048608 | tf_op jit(solution)/shard_map/all_to_all | solution.py:180
  73.5 2.3 slice.69
  75.8 4.7 %all-to-all-start.4 = ((f32[32,8,1024]{2,1,0:T(8,128)}), f32[32,8,1024]{2,1,0:T(8,128)}, u32[]{:S(2)}, u32[]{:S(2)}) async-start(f32[32,8,1024]{2,1,0:T(8,128)} %bitcast.15), calls=%async_computation.4 | async-start | bytes 2097152 | tf_op jit(solution)/shard_map/all_to_all | solution.py:180
  80.5 13.5 %split_ladder.1 = (bf16[8,1024,512]{2,1,0:T(8,128)(2,1)S(1)}, bf16[8,1024,512]{2,1,0:T(8,128)(2,1)}) custom-call(s32[8]{0:T(128)S(1)} %broadcast_subtract_fusion.count_ref, f32[8,512,1024]{2,1,0:T(8,128)} %ladder_ref.1), custom_call_target="tpu_custom_call" | custom-call | flops 33554432 | bytes 33554432 | tf_op jit(solution)/shard_map/split_ladder/pallas_call | solution.py:33
  93.9 3.3 %copy-done.4 = bf16[8,1024,512]{2,1,0:T(8,128)(2,1)} copy-done((bf16[8,1024,512]{2,1,0:T(8,128)(2,1)}, bf16[8,1024,512]{2,1,0:T(8,128)(2,1)S(1)}, u32[]{:S(2)}) %copy-start.4) | copy-done | bytes 8388632
  98.8 1.7 collective-permute-start.10
  100.6 1.9 slice.82
  102.8 1.9 slice.83
  104.7 3.0 collective-permute-start.8
  107.6 16.5 %ladder_products.5 = (f32[16,32,512]{2,1,0:T(8,128)S(1)}, f32[16,32,512]{2,1,0:T(8,128)}) custom-call(s32[9]{0:T(128)S(1)} %get-tuple-element.91.bound_ref, s32[2]{0:T(128)S(1)} %pad_add_fusion.place_ref, f32[256,1024]{1,0:T(8,128)S(1)} %bitcast.54, f32[256,1024]{1,0:T(8,128)} %collective-permute-done.left, f32[256,1024]{1,0:T(8,128)} %collective-permute-done.1.right, ...), custom_call_target="tpu_custom_call" | custom-call | flops 6442450944 | bytes 23068672 | tf_op jit(solution)/shard_map/ladder_products/pallas_call | solution.py:128
  124.3 2.3 slice.73
  126.5 7.5 %all-to-all-start.6 = ((f32[32,8,1024]{2,1,0:T(8,128)}), f32[32,8,1024]{2,1,0:T(8,128)}, u32[]{:S(2)}, u32[]{:S(2)}) async-start(f32[32,8,1024]{2,1,0:T(8,128)} %bitcast.56), calls=%async_computation.6 | async-start | bytes 2097152 | tf_op jit(solution)/shard_map/all_to_all | solution.py:180
  135.3 3.0 collective-permute-start.15
  138.3 1.9 slice.84
  140.2 1.9 slice.85
  142.1 3.2 %collective-permute-start.13 = (f32[128,1024]{1,0:T(8,128)}, f32[128,1024]{1,0:T(8,128)}, u32[]{:S(2)}, u32[]{:S(2)}) collective-permute-start(f32[128,1024]{1,0:T(8,128)} %slice.85), channel_id=1, source_target_pairs={{0,96},{32,0},{64,32},{96,64},{1,97},{33,1},{65,33},{97,65},{2,98}... | collective-permute-start | bytes 1572872 | tf_op jit(solution)/shard_map/ppermute | solution.py:184
  148.6 12.3 %ladder_products.6 = (f32[16,32,512]{2,1,0:T(8,128)S(1)}, f32[16,32,512]{2,1,0:T(8,128)}) custom-call(s32[9]{0:T(128)S(1)} %get-tuple-element.88.bound_ref, s32[2]{0:T(128)S(1)} %pad_add_fusion.place_ref, f32[256,1024]{1,0:T(8,128)S(1)} %bitcast.51, f32[256,1024]{1,0:T(8,128)} %collective-permute-done.4.left, f32[256,1024]{1,0:T(8,128)} %collective-permute-done.5.right, ...), custom_call_target="tpu_custom_call" | custom-call | flops 6442450944 | bytes 23068672 | tf_op jit(solution)/shard_map/ladder_products/pallas_call | solution.py:128
  161.1 2.4 add.75
  163.5 7.1 %all-to-all-start.3 = ((f32[16,32,512]{2,1,0:T(8,128)}), f32[16,32,512]{2,1,0:T(8,128)}, u32[]{:S(2)}, u32[]{:S(2)}) async-start(f32[16,32,512]{2,1,0:T(8,128)} %add.75), calls=%async_computation.3 | async-start | bytes 2097152 | tf_op jit(solution)/shard_map/all_to_all | solution.py:199
  172.2 3.2 %collective-permute-start.20 = (f32[256,1024]{1,0:T(8,128)}, f32[256,1024]{1,0:T(8,128)}, u32[]{:S(2)}, u32[]{:S(2)}) collective-permute-start(f32[256,1024]{1,0:T(8,128)} %bitcast.21.own), channel_id=1, source_target_pairs={{0,96},{32,0},{64,32},{96,64},{1,97},{33,1},{65,33},{97,65},{2,98}... | collective-permute-start | bytes 3145736 | tf_op jit(solution)/shard_map/ppermute | solution.py:184
  175.4 1.9 slice.86
  177.3 1.9 slice.87
  179.2 3.2 %collective-permute-start.18 = (f32[128,1024]{1,0:T(8,128)}, f32[128,1024]{1,0:T(8,128)}, u32[]{:S(2)}, u32[]{:S(2)}) collective-permute-start(f32[128,1024]{1,0:T(8,128)} %slice.87), channel_id=1, source_target_pairs={{0,96},{32,0},{64,32},{96,64},{1,97},{33,1},{65,33},{97,65},{2,98}... | collective-permute-start | bytes 1572872 | tf_op jit(solution)/shard_map/ppermute | solution.py:184
  182.5 16.5 %ladder_products.7 = (f32[16,32,512]{2,1,0:T(8,128)S(1)}, f32[16,32,512]{2,1,0:T(8,128)}) custom-call(s32[9]{0:T(128)S(1)} %get-tuple-element.89.bound_ref, s32[2]{0:T(128)S(1)} %pad_add_fusion.place_ref, f32[256,1024]{1,0:T(8,128)S(1)} %bitcast.48, f32[256,1024]{1,0:T(8,128)} %collective-permute-done.9.left, f32[256,1024]{1,0:T(8,128)} %collective-permute-done.10.right, ...), custom_call_target="tpu_custom_call" | custom-call | flops 6442450944 | bytes 23068672 | tf_op jit(solution)/shard_map/ladder_products/pallas_call | solution.py:128
  199.0 2.4 add.76
  201.5 7.0 %all-to-all-start.5 = ((f32[16,32,512]{2,1,0:T(8,128)}), f32[16,32,512]{2,1,0:T(8,128)}, u32[]{:S(2)}, u32[]{:S(2)}) async-start(f32[16,32,512]{2,1,0:T(8,128)} %add.76), calls=%async_computation.5 | async-start | bytes 2097152 | tf_op jit(solution)/shard_map/all_to_all | solution.py:199
  209.9 1.9 slice.88
  211.8 1.9 slice.89
  213.7 3.2 %collective-permute-start.23 = (f32[128,1024]{1,0:T(8,128)}, f32[128,1024]{1,0:T(8,128)}, u32[]{:S(2)}, u32[]{:S(2)}) collective-permute-start(f32[128,1024]{1,0:T(8,128)} %slice.89), channel_id=1, source_target_pairs={{0,96},{32,0},{64,32},{96,64},{1,97},{33,1},{65,33},{97,65},{2,98}... | collective-permute-start | bytes 1572872 | tf_op jit(solution)/shard_map/ppermute | solution.py:184
  216.9 17.7 %ladder_products.8 = (f32[16,32,512]{2,1,0:T(8,128)S(1)}, f32[16,32,512]{2,1,0:T(8,128)S(1)}) custom-call(s32[9]{0:T(128)S(1)} %get-tuple-element.90.bound_ref, s32[2]{0:T(128)S(1)} %pad_add_fusion.place_ref, f32[256,1024]{1,0:T(8,128)} %bitcast.16.own, f32[256,1024]{1,0:T(8,128)} %collective-permute-done.14.left, ...), custom_call_target="tpu_custom_call" | custom-call | flops 6442450944 | bytes 23068672 | tf_op jit(solution)/shard_map/ladder_products/pallas_call | solution.py:128
  234.7 2.4 add.77
  237.2 7.2 %all-to-all-start.7 = ((f32[16,32,512]{2,1,0:T(8,128)}), f32[16,32,512]{2,1,0:T(8,128)}, u32[]{:S(2)}, u32[]{:S(2)}) async-start(f32[16,32,512]{2,1,0:T(8,128)} %add.77), calls=%async_computation.7 | async-start | bytes 2097152 | tf_op jit(solution)/shard_map/all_to_all | solution.py:199
  245.7 16.7 %ladder_products.9 = (f32[16,32,512]{2,1,0:T(8,128)S(1)}, f32[16,32,512]{2,1,0:T(8,128)}) custom-call(s32[9]{0:T(128)S(1)} %get-tuple-element.87.bound_ref, s32[2]{0:T(128)S(1)} %pad_add_fusion.place_ref, f32[256,1024]{1,0:T(8,128)} %bitcast.21.own, f32[256,1024]{1,0:T(8,128)} %collective-permute-done.19.left, f32[256,1024]{1,0:T(8,128)} %collective-permute-done.20.right, ...), custom_call_target="tpu_custom_call" | custom-call | flops 6442450944 | bytes 23068672 | tf_op jit(solution)/shard_map/ladder_products/pallas_call | solution.py:128
  262.7 2.4 add.78
  265.1 7.0 %all-to-all-start.8 = ((f32[16,32,512]{2,1,0:T(8,128)}), f32[16,32,512]{2,1,0:T(8,128)S(1)}, u32[]{:S(2)}, u32[]{:S(2)}) async-start(f32[16,32,512]{2,1,0:T(8,128)} %add.78), calls=%async_computation.8 | async-start | bytes 2097152 | tf_op jit(solution)/shard_map/all_to_all | solution.py:199
  273.3 2.4 add.79
  275.8 14.8 %all-to-all-done.8 = f32[16,32,512]{2,1,0:T(8,128)S(1)} async-done(((f32[16,32,512]{2,1,0:T(8,128)}), f32[16,32,512]{2,1,0:T(8,128)S(1)}, u32[]{:S(2)}, u32[]{:S(2)}) %all-to-all-start.8) | async-done | bytes 1048608 | tf_op jit(solution)/shard_map/all_to_all | solution.py:199
  290.6 3.7 %all-to-all-start.9 = ((f32[16,32,512]{2,1,0:T(8,128)}), f32[16,32,512]{2,1,0:T(8,128)S(1)}, u32[]{:S(2)}, u32[]{:S(2)}) async-start(f32[16,32,512]{2,1,0:T(8,128)} %add.79), calls=%async_computation.9 | async-start | bytes 2097152 | tf_op jit(solution)/shard_map/all_to_all | solution.py:199
  295.7 14.9 %all-to-all-done.9 = f32[16,32,512]{2,1,0:T(8,128)S(1)} async-done(((f32[16,32,512]{2,1,0:T(8,128)}), f32[16,32,512]{2,1,0:T(8,128)S(1)}, u32[]{:S(2)}, u32[]{:S(2)}) %all-to-all-start.9) | async-done | bytes 1048608 | tf_op jit(solution)/shard_map/all_to_all | solution.py:199
  (98 shorter events, 23.3 us)
Async XLA Ops:
  1.3 58.7 %copy-start.12 = (s32[8]{0:T(128)S(1)}, s32[8]{0:T(128)}, u32[]{:S(2)}) copy-start(s32[8]{0:T(128)} %param.10) | copy-start | bytes 100
  26.3 37.8 %copy-start.2 = (f32[32,8,1024]{2,1,0:T(8,128)}, f32[32,8,1024]{2,1,0:T(8,128)S(1)}, u32[]{:S(2)}) copy-start(f32[32,8,1024]{2,1,0:T(8,128)S(1)} %all_to_all.50) | copy-start | bytes 3145732
  29.0 20.9 %all-to-all-start.1 = ((f32[32,8,1024]{2,1,0:T(8,128)}), f32[32,8,1024]{2,1,0:T(8,128)S(1)}, u32[]{:S(2)}, u32[]{:S(2)}) async-start(f32[32,8,1024]{2,1,0:T(8,128)} %bitcast.7), calls=%async_computation.1 | async-start | bytes 2097152 | tf_op jit(solution)/shard_map/all_to_all | solution.py:180
  33.1 27.0 %collective-permute-start = (f32[256,1024]{1,0:T(8,128)S(1)}, f32[256,1024]{1,0:T(8,128)}, u32[]{:S(2)}, u32[]{:S(2)}) collective-permute-start(f32[256,1024]{1,0:T(8,128)S(1)} %bitcast.52), channel_id=1, source_target_pairs={{0,32},{32,64},{64,96},{96,0},{1,33},{33,65},{65,97},{97,1},{2,34}... | collective-permute-start | bytes 3145736 | tf_op jit(solution)/shard_map/ppermute | solution.py:184
  34.6 27.7 %collective-permute-start.1 = (f32[256,1024]{1,0:T(8,128)S(1)}, f32[256,1024]{1,0:T(8,128)}, u32[]{:S(2)}, u32[]{:S(2)}) collective-permute-start(f32[256,1024]{1,0:T(8,128)S(1)} %bitcast.53), channel_id=1, source_target_pairs={{0,96},{32,0},{64,32},{96,64},{1,97},{33,1},{65,33},{97,65},{2,98}... | collective-permute-start | bytes 3145736 | tf_op jit(solution)/shard_map/ppermute | solution.py:184
  49.9 25.9 %copy-start = (f32[32,8,1024]{2,1,0:T(8,128)}, f32[32,8,1024]{2,1,0:T(8,128)S(1)}, u32[]{:S(2)}) copy-start(f32[32,8,1024]{2,1,0:T(8,128)S(1)} %all-to-all-done.1) | copy-start | bytes 3145732
  49.9 30.6 %copy-start.11 = (s32[8]{0:T(128)S(1)}, s32[8]{0:T(128)}, u32[]{:S(2)}) copy-start(s32[8]{0:T(128)} %param.11) | copy-start | bytes 100
  52.6 20.9 %all-to-all-start.2 = ((f32[32,8,1024]{2,1,0:T(8,128)}), f32[32,8,1024]{2,1,0:T(8,128)S(1)}, u32[]{:S(2)}, u32[]{:S(2)}) async-start(f32[32,8,1024]{2,1,0:T(8,128)} %bitcast.55), calls=%async_computation.2 | async-start | bytes 2097152 | tf_op jit(solution)/shard_map/all_to_all | solution.py:180
  56.6 44.0 %collective-permute-start.4 = (f32[256,1024]{1,0:T(8,128)S(1)}, f32[256,1024]{1,0:T(8,128)}, u32[]{:S(2)}, u32[]{:S(2)}) collective-permute-start(f32[256,1024]{1,0:T(8,128)S(1)} %bitcast.49), channel_id=1, source_target_pairs={{0,32},{32,64},{64,96},{96,0},{1,33},{33,65},{65,97},{97,1},{2,34}... | collective-permute-start | bytes 3145736 | tf_op jit(solution)/shard_map/ppermute | solution.py:184
  58.2 42.4 %collective-permute-start.5 = (f32[256,1024]{1,0:T(8,128)S(1)}, f32[256,1024]{1,0:T(8,128)}, u32[]{:S(2)}, u32[]{:S(2)}) collective-permute-start(f32[256,1024]{1,0:T(8,128)S(1)} %bitcast.50), channel_id=1, source_target_pairs={{0,96},{32,0},{64,32},{96,64},{1,97},{33,1},{65,33},{97,65},{2,98}... | collective-permute-start | bytes 3145736 | tf_op jit(solution)/shard_map/ppermute | solution.py:184
  62.0 36.8 %collective-permute-start.2 = (f32[128,1024]{1,0:T(8,128)}, f32[128,1024]{1,0:T(8,128)}, u32[]{:S(2)}, u32[]{:S(2)}) collective-permute-start(f32[128,1024]{1,0:T(8,128)} %slice.80), channel_id=1, source_target_pairs={{0,32},{32,64},{64,96},{96,0},{1,33},{33,65},{65,97},{97,1},{2,34}... | collective-permute-start | bytes 1572872 | tf_op jit(solution)/shard_map/ppermute | solution.py:184
  64.2 36.4 %collective-permute-start.3 = (f32[128,1024]{1,0:T(8,128)}, f32[128,1024]{1,0:T(8,128)}, u32[]{:S(2)}, u32[]{:S(2)}) collective-permute-start(f32[128,1024]{1,0:T(8,128)} %slice.81), channel_id=1, source_target_pairs={{0,96},{32,0},{64,32},{96,64},{1,97},{33,1},{65,33},{97,65},{2,98}... | collective-permute-start | bytes 1572872 | tf_op jit(solution)/shard_map/ppermute | solution.py:184
  75.8 48.5 %all-to-all-start.4 = ((f32[32,8,1024]{2,1,0:T(8,128)}), f32[32,8,1024]{2,1,0:T(8,128)}, u32[]{:S(2)}, u32[]{:S(2)}) async-start(f32[32,8,1024]{2,1,0:T(8,128)} %bitcast.15), calls=%async_computation.4 | async-start | bytes 2097152 | tf_op jit(solution)/shard_map/all_to_all | solution.py:180
  80.5 27.2 %copy-start.3 = (f32[32,8,1024]{2,1,0:T(8,128)S(1)}, f32[32,8,1024]{2,1,0:T(8,128)}, u32[]{:S(2)}) copy-start(f32[32,8,1024]{2,1,0:T(8,128)} %copy-done.2) | copy-start | bytes 3145732
  93.9 3.3 %copy-start.4 = (bf16[8,1024,512]{2,1,0:T(8,128)(2,1)}, bf16[8,1024,512]{2,1,0:T(8,128)(2,1)S(1)}, u32[]{:S(2)}) copy-start(bf16[8,1024,512]{2,1,0:T(8,128)(2,1)S(1)} %get-tuple-element.53.high) | copy-start | bytes 25165828
  97.3 40.9 %collective-permute-start.9 = (f32[256,1024]{1,0:T(8,128)S(1)}, f32[256,1024]{1,0:T(8,128)}, u32[]{:S(2)}, u32[]{:S(2)}) collective-permute-start(f32[256,1024]{1,0:T(8,128)S(1)} %bitcast.46), channel_id=1, source_target_pairs={{0,32},{32,64},{64,96},{96,0},{1,33},{33,65},{65,97},{97,1},{2,34}... | collective-permute-start | bytes 3145736 | tf_op jit(solution)/shard_map/ppermute | solution.py:184
  98.8 39.4 %collective-permute-start.10 = (f32[256,1024]{1,0:T(8,128)S(1)}, f32[256,1024]{1,0:T(8,128)}, u32[]{:S(2)}, u32[]{:S(2)}) collective-permute-start(f32[256,1024]{1,0:T(8,128)S(1)} %bitcast.47), channel_id=1, source_target_pairs={{0,96},{32,0},{64,32},{96,64},{1,97},{33,1},{65,33},{97,65},{2,98}... | collective-permute-start | bytes 3145736 | tf_op jit(solution)/shard_map/ppermute | solution.py:184
  102.5 32.5 %collective-permute-start.7 = (f32[128,1024]{1,0:T(8,128)}, f32[128,1024]{1,0:T(8,128)S(1)}, u32[]{:S(2)}, u32[]{:S(2)}) collective-permute-start(f32[128,1024]{1,0:T(8,128)} %slice.82), channel_id=1, source_target_pairs={{0,32},{32,64},{64,96},{96,0},{1,33},{33,65},{65,97},{97,1},{2,34}... | collective-permute-start | bytes 1572872 | tf_op jit(solution)/shard_map/ppermute | solution.py:184
  104.7 30.6 %collective-permute-start.8 = (f32[128,1024]{1,0:T(8,128)}, f32[128,1024]{1,0:T(8,128)S(1)}, u32[]{:S(2)}, u32[]{:S(2)}) collective-permute-start(f32[128,1024]{1,0:T(8,128)} %slice.83), channel_id=1, source_target_pairs={{0,96},{32,0},{64,32},{96,64},{1,97},{33,1},{65,33},{97,65},{2,98}... | collective-permute-start | bytes 1572872 | tf_op jit(solution)/shard_map/ppermute | solution.py:184
  124.2 36.8 %collective-permute-start.6 = (f32[16,32,512]{2,1,0:T(8,128)}, f32[16,32,512]{2,1,0:T(8,128)}, u32[]{:S(2)}, u32[]{:S(2)}) collective-permute-start(f32[16,32,512]{2,1,0:T(8,128)} %get-tuple-element.56), channel_id=1, source_target_pairs={{0,1},{1,0},{2,3},{3,2},{4,5},{5,4},{6,7},{7,6},{8,9},{9,8},{10,11... | collective-permute-start | bytes 3145736 | tf_op jit(solution)/shard_map/ppermute | solution.py:197
  126.5 36.9 %all-to-all-start.6 = ((f32[32,8,1024]{2,1,0:T(8,128)}), f32[32,8,1024]{2,1,0:T(8,128)}, u32[]{:S(2)}, u32[]{:S(2)}) async-start(f32[32,8,1024]{2,1,0:T(8,128)} %bitcast.56), calls=%async_computation.6 | async-start | bytes 2097152 | tf_op jit(solution)/shard_map/all_to_all | solution.py:180
  135.0 10.3 %copy-start.5 = (f32[128,1024]{1,0:T(8,128)}, f32[128,1024]{1,0:T(8,128)S(1)}, u32[]{:S(2)}) copy-start(f32[128,1024]{1,0:T(8,128)S(1)} %collective-permute-done.7.far_a) | copy-start | bytes 1572868
  135.0 40.4 %collective-permute-start.14 = (f32[256,1024]{1,0:T(8,128)}, f32[256,1024]{1,0:T(8,128)}, u32[]{:S(2)}, u32[]{:S(2)}) collective-permute-start(f32[256,1024]{1,0:T(8,128)} %bitcast.16.own), channel_id=1, source_target_pairs={{0,32},{32,64},{64,96},{96,0},{1,33},{33,65},{65,97},{97,1},{2,34}... | collective-permute-start | bytes 3145736 | tf_op jit(solution)/shard_map/ppermute | solution.py:184
  135.3 10.0 %copy-start.7 = (f32[128,1024]{1,0:T(8,128)}, f32[128,1024]{1,0:T(8,128)S(1)}, u32[]{:S(2)}) copy-start(f32[128,1024]{1,0:T(8,128)S(1)} %collective-permute-done.8.far_b) | copy-start | bytes 1572868
  135.3 40.1 %collective-permute-start.15 = (f32[256,1024]{1,0:T(8,128)}, f32[256,1024]{1,0:T(8,128)}, u32[]{:S(2)}, u32[]{:S(2)}) collective-permute-start(f32[256,1024]{1,0:T(8,128)} %bitcast.16.own), channel_id=1, source_target_pairs={{0,96},{32,0},{64,32},{96,64},{1,97},{33,1},{65,33},{97,65},{2,98}... | collective-permute-start | bytes 3145736 | tf_op jit(solution)/shard_map/ppermute | solution.py:184
  140.2 32.0 %collective-permute-start.12 = (f32[128,1024]{1,0:T(8,128)}, f32[128,1024]{1,0:T(8,128)}, u32[]{:S(2)}, u32[]{:S(2)}) collective-permute-start(f32[128,1024]{1,0:T(8,128)} %slice.84), channel_id=1, source_target_pairs={{0,32},{32,64},{64,96},{96,0},{1,33},{33,65},{65,97},{97,1},{2,34}... | collective-permute-start | bytes 1572872 | tf_op jit(solution)/shard_map/ppermute | solution.py:184
  142.1 30.1 %collective-permute-start.13 = (f32[128,1024]{1,0:T(8,128)}, f32[128,1024]{1,0:T(8,128)}, u32[]{:S(2)}, u32[]{:S(2)}) collective-permute-start(f32[128,1024]{1,0:T(8,128)} %slice.85), channel_id=1, source_target_pairs={{0,96},{32,0},{64,32},{96,64},{1,97},{33,1},{65,33},{97,65},{2,98}... | collective-permute-start | bytes 1572872 | tf_op jit(solution)/shard_map/ppermute | solution.py:184
  145.3 1.2 copy-start.1
  146.5 1.0 copy-start.6
  147.6 1.0 copy-start.8
  161.0 38.0 %collective-permute-start.11 = (f32[16,32,512]{2,1,0:T(8,128)}, f32[16,32,512]{2,1,0:T(8,128)}, u32[]{:S(2)}, u32[]{:S(2)}) collective-permute-start(f32[16,32,512]{2,1,0:T(8,128)} %get-tuple-element.64), channel_id=1, source_target_pairs={{0,1},{1,0},{2,3},{3,2},{4,5},{5,4},{6,7},{7,6},{8,9},{9,8},{10,11... | collective-permute-start | bytes 3145736 | tf_op jit(solution)/shard_map/ppermute | solution.py:197
  163.5 38.0 %all-to-all-start.3 = ((f32[16,32,512]{2,1,0:T(8,128)}), f32[16,32,512]{2,1,0:T(8,128)}, u32[]{:S(2)}, u32[]{:S(2)}) async-start(f32[16,32,512]{2,1,0:T(8,128)} %add.75), calls=%async_computation.3 | async-start | bytes 2097152 | tf_op jit(solution)/shard_map/all_to_all | solution.py:199
  172.2 37.6 %collective-permute-start.19 = (f32[256,1024]{1,0:T(8,128)}, f32[256,1024]{1,0:T(8,128)}, u32[]{:S(2)}, u32[]{:S(2)}) collective-permute-start(f32[256,1024]{1,0:T(8,128)} %bitcast.21.own), channel_id=1, source_target_pairs={{0,32},{32,64},{64,96},{96,0},{1,33},{33,65},{65,97},{97,1},{2,34}... | collective-permute-start | bytes 3145736 | tf_op jit(solution)/shard_map/ppermute | solution.py:184
  172.2 37.7 %collective-permute-start.20 = (f32[256,1024]{1,0:T(8,128)}, f32[256,1024]{1,0:T(8,128)}, u32[]{:S(2)}, u32[]{:S(2)}) collective-permute-start(f32[256,1024]{1,0:T(8,128)} %bitcast.21.own), channel_id=1, source_target_pairs={{0,96},{32,0},{64,32},{96,64},{1,97},{33,1},{65,33},{97,65},{2,98}... | collective-permute-start | bytes 3145736 | tf_op jit(solution)/shard_map/ppermute | solution.py:184
  177.3 32.5 %collective-permute-start.17 = (f32[128,1024]{1,0:T(8,128)}, f32[128,1024]{1,0:T(8,128)}, u32[]{:S(2)}, u32[]{:S(2)}) collective-permute-start(f32[128,1024]{1,0:T(8,128)} %slice.86), channel_id=1, source_target_pairs={{0,32},{32,64},{64,96},{96,0},{1,33},{33,65},{65,97},{97,1},{2,34}... | collective-permute-start | bytes 1572872 | tf_op jit(solution)/shard_map/ppermute | solution.py:184
  179.2 30.6 %collective-permute-start.18 = (f32[128,1024]{1,0:T(8,128)}, f32[128,1024]{1,0:T(8,128)}, u32[]{:S(2)}, u32[]{:S(2)}) collective-permute-start(f32[128,1024]{1,0:T(8,128)} %slice.87), channel_id=1, source_target_pairs={{0,96},{32,0},{64,32},{96,64},{1,97},{33,1},{65,33},{97,65},{2,98}... | collective-permute-start | bytes 1572872 | tf_op jit(solution)/shard_map/ppermute | solution.py:184
  198.9 35.8 %collective-permute-start.16 = (f32[16,32,512]{2,1,0:T(8,128)}, f32[16,32,512]{2,1,0:T(8,128)}, u32[]{:S(2)}, u32[]{:S(2)}) collective-permute-start(f32[16,32,512]{2,1,0:T(8,128)} %get-tuple-element.72), channel_id=1, source_target_pairs={{0,1},{1,0},{2,3},{3,2},{4,5},{5,4},{6,7},{7,6},{8,9},{9,8},{10,11... | collective-permute-start | bytes 3145736 | tf_op jit(solution)/shard_map/ppermute | solution.py:197
  201.5 35.7 %all-to-all-start.5 = ((f32[16,32,512]{2,1,0:T(8,128)}), f32[16,32,512]{2,1,0:T(8,128)}, u32[]{:S(2)}, u32[]{:S(2)}) async-start(f32[16,32,512]{2,1,0:T(8,128)} %add.76), calls=%async_computation.5 | async-start | bytes 2097152 | tf_op jit(solution)/shard_map/all_to_all | solution.py:199
  211.8 33.9 %collective-permute-start.22 = (f32[128,1024]{1,0:T(8,128)}, f32[128,1024]{1,0:T(8,128)}, u32[]{:S(2)}, u32[]{:S(2)}) collective-permute-start(f32[128,1024]{1,0:T(8,128)} %slice.88), channel_id=1, source_target_pairs={{0,32},{32,64},{64,96},{96,0},{1,33},{33,65},{65,97},{97,1},{2,34}... | collective-permute-start | bytes 1572872 | tf_op jit(solution)/shard_map/ppermute | solution.py:184
  213.7 32.0 %collective-permute-start.23 = (f32[128,1024]{1,0:T(8,128)}, f32[128,1024]{1,0:T(8,128)}, u32[]{:S(2)}, u32[]{:S(2)}) collective-permute-start(f32[128,1024]{1,0:T(8,128)} %slice.89), channel_id=1, source_target_pairs={{0,96},{32,0},{64,32},{96,64},{1,97},{33,1},{65,33},{97,65},{2,98}... | collective-permute-start | bytes 1572872 | tf_op jit(solution)/shard_map/ppermute | solution.py:184
  234.6 28.1 %collective-permute-start.21 = (f32[16,32,512]{2,1,0:T(8,128)S(1)}, f32[16,32,512]{2,1,0:T(8,128)}, u32[]{:S(2)}, u32[]{:S(2)}) collective-permute-start(f32[16,32,512]{2,1,0:T(8,128)S(1)} %get-tuple-element.79), channel_id=1, source_target_pairs={{0,1},{1,0},{2,3},{3,2},{4,5},{5,4},{6,7},{7,6},{8,9},{9,8},{10,11... | collective-permute-start | bytes 3145736 | tf_op jit(solution)/shard_map/ppermute | solution.py:197
  237.2 27.9 %all-to-all-start.7 = ((f32[16,32,512]{2,1,0:T(8,128)}), f32[16,32,512]{2,1,0:T(8,128)}, u32[]{:S(2)}, u32[]{:S(2)}) async-start(f32[16,32,512]{2,1,0:T(8,128)} %add.77), calls=%async_computation.7 | async-start | bytes 2097152 | tf_op jit(solution)/shard_map/all_to_all | solution.py:199
  262.4 10.0 %copy-start.9 = (f32[8,512]{1,0:T(8,128)S(1)}, f32[8,512]{1,0:T(8,128)}, u32[]{:S(2)}) copy-start(f32[8,512]{1,0:T(8,128)} %param.9) | copy-start | bytes 49156
  262.4 10.9 %collective-permute-start.24 = (f32[16,32,512]{2,1,0:T(8,128)}, f32[16,32,512]{2,1,0:T(8,128)}, u32[]{:S(2)}, u32[]{:S(2)}) collective-permute-start(f32[16,32,512]{2,1,0:T(8,128)} %get-tuple-element.86), channel_id=1, source_target_pairs={{0,1},{1,0},{2,3},{3,2},{4,5},{5,4},{6,7},{7,6},{8,9},{9,8},{10,11... | collective-permute-start | bytes 3145736 | tf_op jit(solution)/shard_map/ppermute | solution.py:197
  265.1 25.4 %all-to-all-start.8 = ((f32[16,32,512]{2,1,0:T(8,128)}), f32[16,32,512]{2,1,0:T(8,128)S(1)}, u32[]{:S(2)}, u32[]{:S(2)}) async-start(f32[16,32,512]{2,1,0:T(8,128)} %add.78), calls=%async_computation.8 | async-start | bytes 2097152 | tf_op jit(solution)/shard_map/all_to_all | solution.py:199
  272.1 38.6 %copy-start.10 = (f32[160]{0:T(256)S(1)}, f32[160]{0:T(256)}, u32[]{:S(2)}) copy-start(f32[160]{0:T(256)} %param.8) | copy-start | bytes 1924
  290.6 20.0 %all-to-all-start.9 = ((f32[16,32,512]{2,1,0:T(8,128)}), f32[16,32,512]{2,1,0:T(8,128)S(1)}, u32[]{:S(2)}, u32[]{:S(2)}) async-start(f32[16,32,512]{2,1,0:T(8,128)} %add.79), calls=%async_computation.9 | async-start | bytes 2097152 | tf_op jit(solution)/shard_map/all_to_all | solution.py:199

commit v3 on v2

v3 whole, which is shorter than its diff:
```python
import functools

import jax
import jax.numpy as jnp
from jax import lax
from jax.experimental import pallas as pl
from jax.experimental.pallas import tpu as pltpu
from jax.sharding import Mesh, PartitionSpec as P

STEP = 8
TILE = 128
CORES = 2
UNITS = (1, 1, 1, 1, 1)
AHEAD = 2
EARLY = 2
JOINS = (1, 2, 3, 4, 5)
DIRECT = False
HALVES = True


def split(value):
    high = value.astype(jnp.bfloat16)
    return high, (value - high.astype(jnp.float32)).astype(jnp.bfloat16)


def split_kernel(count_ref, ladder_ref, high_ref, low_ref):
    group = pl.program_id(0)
    value = ladder_ref[0]
    column = lax.broadcasted_iota(jnp.int32, value.shape, 1)
    value = jnp.where(column < count_ref[group], value, jnp.float32(0.0))
    high, low = split(value.T)
    high_ref[0] = high
    low_ref[0] = low


def split_ladder(ladder, counts):
    groups, rows, cols = ladder.shape
    spec = pl.BlockSpec((1, rows, cols), lambda g, c: (g, 0, 0))
    turned = pl.BlockSpec((1, cols, rows), lambda g, c: (g, 0, 0))
    half = jax.ShapeDtypeStruct((groups, cols, rows), jnp.bfloat16)
    return pl.pallas_call(
        split_kernel,
        grid_spec=pltpu.PrefetchScalarGridSpec(
            num_scalar_prefetch=1, grid=(groups,), in_specs=[spec], out_specs=[turned, turned]
        ),
        out_shape=[half, half],
        compiler_params=pltpu.CompilerParams(vmem_limit_bytes=60 << 20),
        cost_estimate=pl.CostEstimate(flops=8 * ladder.size, transcendentals=0, bytes_accessed=4 * ladder.size),
        name="split_ladder",
    )(counts, ladder)


def product_kernel(bound_ref, place_ref, *refs, steps):
    parts = refs[: len(steps)]
    high_ref, low_ref, *targets, rows, out, high, low, row_sems, weight_sems, out_sems = refs[len(steps) :]
    mine, other = targets if len(targets) == 2 else (targets[0], None)
    groups = high.shape[0]
    blocks, sets, step_rows, cols = rows.shape
    unit = sets * step_rows
    tile = TILE // unit
    x, core = place_ref[0], place_ref[1]
    planes = place_ref[2]

    copies = []
    for i, (part, (step, offset, which)) in enumerate(zip(parts, steps)):
        start = lax.rem(x + step, planes) * lax.div(blocks, planes) + offset
        copies.append(
            pltpu.make_async_copy(part, rows.at[pl.ds(start, part.shape[0]), which], row_sems.at[i])
        )
    for copy in copies:
        copy.start()

    def fetch(group):
        return [
            pltpu.make_async_copy(source.at[group], target.at[group], weight_sems.at[i, group])
            for i, (source, target) in enumerate([(high_ref, high), (low_ref, low)])
        ]

    for group in range(AHEAD):
        for copy in fetch(group):
            copy.start()
    for copy in copies:
        copy.wait()

    def times(a, b):
        return lax.dot_general(a, b, (((1,), (0,)), ((), ())), preferred_element_type=jnp.float32)

    for group in range(groups):
        for copy in fetch(group):
            copy.wait()
        if group + AHEAD < groups:
            for copy in fetch(group + AHEAD):
                copy.start()
        first, last = bound_ref[group], bound_ref[group + 1]
        start = lax.div(first, unit)
        number = jnp.where(last > first, lax.div(last - start * unit + (TILE - 1), TILE), 0)

        def visit(turn, carry, group=group, first=first, last=last, start=start):
            at = jnp.minimum(start + turn * tile, blocks - tile)
            a_high, a_low = split(rows[pl.ds(at, tile)].reshape(TILE, cols))
            weights = high[group]
            product = times(a_low, weights) + times(a_high, low[group]) + times(a_high, weights)
            row = lax.broadcasted_iota(jnp.int32, product.shape, 0) + at * unit
            kept = out[pl.ds(at, tile)].reshape(product.shape)
            product = jnp.where((row >= first) & (row < last), product, kept)
            out[pl.ds(at, tile)] = product.reshape(tile, sets, step_rows, product.shape[1])
            return carry

        lax.fori_loop(0, number, visit, 0)

    if other is None:
        copy = pltpu.make_async_copy(out, mine, out_sems.at[0, 0])
        copy.start()
        copy.wait()
        return
    pieces, piece_blocks = mine.shape[:2]
    copies = []
    for piece in range(pieces):
        for kind, (target, which) in enumerate([(other, 1 - core), (mine, core)]):
            start = (piece * CORES + which) * piece_blocks
            copy = pltpu.make_async_copy(
                out.at[pl.ds(start, piece_blocks)], target.at[piece], out_sems.at[kind, piece]
            )
            copy.start()
            copies.append(copy)
    for copy in copies:
        copy.wait()


def products(bound, place, parts, steps, high, low, pieces, blocks, sets, whole):
    groups, cols, ab = high.shape
    hbm = pl.BlockSpec(memory_space=pltpu.HBM)
    smem = pl.BlockSpec(memory_space=pltpu.SMEM)
    shapes = [jax.ShapeDtypeStruct((pieces, blocks // pieces // CORES, sets, STEP, ab), jnp.float32)] * 2
    if whole:
        shapes = [jax.ShapeDtypeStruct((blocks, sets, STEP, ab), jnp.float32)]
    total = blocks * sets * STEP
    return pl.pallas_call(
        functools.partial(product_kernel, steps=steps),
        in_specs=[smem, smem] + [hbm] * (len(parts) + 2),
        out_specs=[hbm] * len(shapes),
        out_shape=shapes,
        scratch_shapes=[
            pltpu.VMEM((blocks, sets, STEP, cols), jnp.float32),
            pltpu.VMEM((blocks, sets, STEP, ab), jnp.float32),
            pltpu.VMEM((groups, cols, ab), jnp.bfloat16),
            pltpu.VMEM((groups, cols, ab), jnp.bfloat16),
            pltpu.SemaphoreType.DMA((len(parts),)),
            pltpu.SemaphoreType.DMA((2, groups)),
            pltpu.SemaphoreType.DMA((2, pieces)),
        ],
        compiler_params=pltpu.CompilerParams(vmem_limit_bytes=60 << 20),
        cost_estimate=pl.CostEstimate(
            flops=12 * total * ab * cols, transcendentals=0, bytes_accessed=4 * total * (ab + cols)
        ),
        name="ladder_products",
    )(bound, place, *parts, high, low)


def ring(size, step):
    return [(i, (i + step) % size) for i in range(size)]


def after(value, *others):
    return lax.optimization_barrier((value, others))[0]


def body(amplitudes, ladder, pair_energy, vir_energy, occ_count, vir_count):
    groups, ab_local, cd_local = ladder.shape
    rows_x, cols_y, depth = lax.axis_size("row"), lax.axis_size("col"), lax.axis_size("deep")
    plane = cols_y * depth * CORES
    x, core = lax.axis_index("row"), lax.axis_index("core")
    device_pos = lax.axis_index(("col", "deep", "core"))
    block_rows = amplitudes.shape[0]
    chunks = block_rows // STEP
    order = jnp.arange(groups, dtype=jnp.int32)
    ends = jnp.sum(jnp.where(order[None, :] <= order[:, None], occ_count[None, :], 0), axis=1)
    place = jnp.stack([x, core, rows_x]).astype(jnp.int32)
    high, low = split_ladder(ladder, vir_count - device_pos * cd_local)

    spreads = []
    for chunk in range(chunks):
        rows = amplitudes
        if chunk:
            rows = after(rows, spreads[-1], *([high] if chunk == EARLY else []))
        own = rows[chunk * STEP : (chunk + 1) * STEP].reshape(STEP, plane, cd_local).transpose(1, 0, 2)
        spread = lax.all_to_all(own, ("col", "deep", "core"), split_axis=0, concat_axis=0, tiled=True)
        spreads.append(spread)

    def pair(left, right):
        return lax.ppermute(left, "row", ring(rows_x, 1)), lax.ppermute(right, "row", ring(rows_x, rows_x - 1))

    near = [pair(spread, spread) for spread in spreads]
    half = plane // 2
    far_last = pair(near[-1][0][:half], near[-1][1][half:])
    parts, shares = [], []
    chunk = 0
    for sets in UNITS:
        inputs, steps = [], []
        for which in range(sets):
            left, right = near[chunk + which]
            inputs += [spreads[chunk + which], left, right]
            steps += [(0, 0, which), (rows_x - 1, 0, which), (1, 0, which)]
        if sets == 1:
            if chunk + 1 == chunks or HALVES:
                last = chunk + 1 == chunks
                inputs += far_last if last else pair(near[chunk][0][:half], near[chunk][1][half:])
                steps += [(2, 0, 0), (2, half, 0)]
            else:
                turn = rows_x - 1 if chunk % 2 else 1
                inputs.append(lax.ppermute(near[chunk][chunk % 2], "row", ring(rows_x, turn)))
                steps.append((2, 0, 0))
        else:
            inputs += pair(near[chunk][0], near[chunk + 1][1])
            steps += [(2, 0, 0), (2, 0, 1)]
        begin = STEP * chunk
        unit = STEP * sets
        bound = unit * (ends // block_rows) + jnp.clip(ends % block_rows - begin, 0, unit)
        bound = jnp.concatenate([jnp.zeros((1,), jnp.int32), bound])
        chunk += sets
        ready = near[chunk : chunk + 1] + spreads[chunk + 1 : chunk + 2] + parts[-2:-1]
        if len(shares) > 1:
            ready += shares[len(parts) - 3 : len(parts) - 2]
        number = len(parts)
        whole = DIRECT and chunk == chunks
        made = products(
            bound, place, after(tuple(inputs), *ready), tuple(steps), high, low,
            cols_y * depth, plane * rows_x, sets, whole,
        )
        if whole:
            part = made[0].reshape(plane, rows_x, sets, STEP, ab_local)
            met = lax.all_to_all(part, ("col", "deep", "core"), split_axis=0, concat_axis=0, tiled=True)
            shares.append(jnp.sum(met, axis=0))
            break
        other = made[1]
        if chunk + 1 == chunks:
            other = after(other, *far_last)
        parts.append(made[0] + lax.ppermute(other, "core", ring(CORES, 1)))
        if number + 1 in JOINS:
            group = parts[len(shares) :]
            if len(group) == 1:
                met = lax.all_to_all(group[0], ("col", "deep"), split_axis=0, concat_axis=0, tiled=True)
                shares.append(jnp.sum(met, axis=0))
            else:
                met = lax.all_to_all(
                    jnp.stack(group, axis=1), ("col", "deep"), split_axis=0, concat_axis=0, tiled=True
                )
                met = jnp.sum(met, axis=0)
                shares += [met[i] for i in range(len(group))]
    share = jnp.concatenate(shares, axis=1).reshape(-1, ab_local)

    rows_local = share.shape[0]
    row_index = device_pos * rows_local + jnp.arange(rows_local, dtype=jnp.int32)
    row_irrep = jnp.sum((row_index[:, None] >= ends[None, :]).astype(jnp.int32), axis=1)
    onehot = row_irrep[:, None] == order[None, :]
    vir_rows = jnp.sum(jnp.where(onehot[:, :, None], vir_energy[None, :, :], jnp.float32(0.0)), axis=1)
    count_rows = jnp.sum(jnp.where(onehot, vir_count[None, :], 0), axis=1)
    ab_index = x * ab_local + jnp.arange(ab_local, dtype=jnp.int32)
    vir_mask = ab_index[None, :] < count_rows[:, None]
    denom = vir_rows - pair_energy[:, None]
    return jnp.where(vir_mask, share / denom, jnp.float32(0.0))


def solution(mesh):
    shape = mesh.devices.shape
    mesh = Mesh(mesh.devices.reshape(shape[0], shape[1], -1, CORES), ("row", "col", "deep", "core"))
    plane = ("col", "deep", "core")
    placed = (
        P(("row", *plane), None),
        P(None, "row", plane),
        P(plane),
        P(None, "row"),
        P(),
        P(),
    )
    return jax.shard_map(
        body, mesh=mesh, in_specs=placed, out_specs=P(plane, "row"), check_vma=False
    )
```

time: 314 us -> 304 us (0.968)
  waiting for transfers between devices: 52.2 us -> 64.4 us
  Pallas kernels: 93.2 us -> 83.5 us
  local copies, waits for them, and re-layouts: 37 us -> 28.2 us
    ppermute x10, waiting for transfers between devices: 2.59 us -> 24.1 us  [pair(): lax.ppermute(left, 'row', ring(rows_x, 1))]
    all_to_all x4, waiting for transfers between devices: 19.8 us -> 7.03 us  [body(): lax.all_to_all(own, ('col', 'deep', 'core'), split_axis=0, concat_axis=0,...]
    pallas_call x5, Pallas kernels: 79.7 us -> 67.3 us  [products(): pl.pallas_call(functools.partial(product_kernel, steps=steps), in_specs=[...]
    unnamed x30 -> x26, local copies, waits for them, and re-layouts: 6.63 us -> 0.85 us
    all_to_all x4, starting transfers between devices: 20.3 us -> 23.7 us  [body(): lax.all_to_all(own, ('col', 'deep', 'core'), split_axis=0, concat_axis=0,...]
    slice x10, local copies, waits for them, and re-layouts: 18.9 us -> 15.7 us  [the longest x4 6.81 us: body(): near[chunk][0][:half]]
    add x6 -> x7, other arithmetic: 12.2 us -> 10.3 us  [the longest x5 10.3 us: body(): parts.append(made[0] + lax.ppermute(other, 'core', ring(CORES, 1)))]
  transfers between devices with their start and end apart: 34 -> 34, of which waited for: 6 -> 9; matrix products, arithmetic and copies ran while one was open for 14% -> 13% of each run, Pallas kernels for 30% -> 28%
where the time goes in v3:
time: 304 us; the launch traced here: 303 us
  Pallas kernels  83.5 us (27%)
  starting transfers between devices  82.9 us (27%)
  waiting for transfers between devices  64.4 us (21%)
  local copies, waits for them, and re-layouts  28.2 us (9%)
  blocking collectives  25 us (8%)
  other arithmetic  18.1 us (6%)
    pallas_call x5, Pallas kernels, products(): pl.pallas_call(functools.partial(product_kernel, steps=steps), in_specs=[...  67.3 us
    all_to_all x5, waiting for transfers between devices, body(): lax.all_to_all(group[0], ('col', 'deep'), split_axis=0, concat_axis=0, ti...  31.1 us
    all_to_all x5, starting transfers between devices, body(): lax.all_to_all(group[0], ('col', 'deep'), split_axis=0, concat_axis=0, ti...  29.8 us
    all_to_all x1, blocking collectives, body(): lax.all_to_all(own, ('col', 'deep', 'core'), split_axis=0, concat_axis=0,...  25 us
    ppermute x10, waiting for transfers between devices, pair(): lax.ppermute(left, 'row', ring(rows_x, 1))  24.1 us
    ppermute x10, starting transfers between devices, pair(): lax.ppermute(right, 'row', ring(rows_x, rows_x - 1))  24 us
    all_to_all x4, starting transfers between devices, body(): lax.all_to_all(own, ('col', 'deep', 'core'), split_axis=0, concat_axis=0,...  23.7 us
    pallas_call x1, Pallas kernels, split_ladder(): pl.pallas_call(split_kernel, grid_spec=pltpu.PrefetchScalarGridSpec(num_s...  16.2 us
  transfers between devices with their start and end apart: 34, of which 9 were waited for; matrix products, arithmetic and copies ran while one was open for 13% of the time, Pallas kernels for 28%

profile of v3, /device:TPU:0, one launch (start us, length us, event | category | flops | bytes accessed | tf_op | source)
XLA Modules:
  0.0 302.5 jit_solution(5883936748610902134)
XLA Ops:
  1.3 25.0 %all_to_all.50.refs_0_ = f32[32,8,1024]{2,1,0:T(8,128)S(1)} all-to-all(f32[32,8,1024]{2,1,0:T(8,128)S(1)} %bitcast.31), channel_id=1, replica_groups=mesh['row'=4,'col'=4,'deep'=4,'core'=2] {'col','deep','core'}, dimensions={0} | all-to-all | bytes 2097152 | tf_op jit(solution)/shard_map/all_to_all | solution.py:187
  26.3 2.6 slice.48
  29.0 4.1 %all-to-all-start.1 = ((f32[32,8,1024]{2,1,0:T(8,128)}), f32[32,8,1024]{2,1,0:T(8,128)S(1)}, u32[]{:S(2)}, u32[]{:S(2)}) async-start(f32[32,8,1024]{2,1,0:T(8,128)} %bitcast.5), calls=%async_computation.1 | async-start | bytes 2097152 | tf_op jit(solution)/shard_map/all_to_all | solution.py:187
  33.0 1.6 collective-permute-start
  34.6 1.7 collective-permute-start.1
  36.9 16.2 %split_ladder.1 = (bf16[8,1024,512]{2,1,0:T(8,128)(2,1)}, bf16[8,1024,512]{2,1,0:T(8,128)(2,1)}) custom-call(s32[8]{0:T(128)} %broadcast_subtract_fusion.count_ref, f32[8,512,1024]{2,1,0:T(8,128)} %ladder_ref.1), custom_call_target="tpu_custom_call" | custom-call | flops 33554432 | bytes 16777216 | tf_op jit(solution)/shard_map/split_ladder/pallas_call | solution.py:41
  53.1 2.6 slice.49
  55.7 7.4 %all-to-all-start.2 = ((f32[32,8,1024]{2,1,0:T(8,128)}), f32[32,8,1024]{2,1,0:T(8,128)S(1)}, u32[]{:S(2)}, u32[]{:S(2)}) async-start(f32[32,8,1024]{2,1,0:T(8,128)} %bitcast.7), calls=%async_computation.2 | async-start | bytes 2097152 | tf_op jit(solution)/shard_map/all_to_all | solution.py:187
  63.4 3.0 collective-permute-start.5
  66.5 1.9 slice.60
  69.6 3.3 %collective-permute-start.3 = (f32[16,8,1024]{2,1,0:T(8,128)S(1)}, f32[16,8,1024]{2,1,0:T(8,128)S(1)}, u32[]{:S(2)}, u32[]{:S(2)}) collective-permute-start(f32[16,8,1024]{2,1,0:T(8,128)S(1)} %slice.61), channel_id=1, source_target_pairs={{0,96},{32,0},{64,32},{96,64},{1,97},{33,1},{65,33},{97,65},{2,98}... | collective-permute-start | bytes 1572872 | tf_op jit(solution)/shard_map/ppermute | solution.py:191
  72.9 7.0 %all-to-all-done.2.refs_0_ = f32[32,8,1024]{2,1,0:T(8,128)S(1)} async-done(((f32[32,8,1024]{2,1,0:T(8,128)}), f32[32,8,1024]{2,1,0:T(8,128)S(1)}, u32[]{:S(2)}, u32[]{:S(2)}) %all-to-all-start.2) | async-done | bytes 1048608 | tf_op jit(solution)/shard_map/all_to_all | solution.py:187
  79.9 2.6 slice.52
  82.6 4.7 %all-to-all-start.4 = ((f32[32,8,1024]{2,1,0:T(8,128)}), f32[32,8,1024]{2,1,0:T(8,128)}, u32[]{:S(2)}, u32[]{:S(2)}) async-start(f32[32,8,1024]{2,1,0:T(8,128)} %bitcast.10), calls=%async_computation.4 | async-start | bytes 2097152 | tf_op jit(solution)/shard_map/all_to_all | solution.py:187
  88.7 13.0 %collective-permute-done.2.refs_3_ = f32[16,8,1024]{2,1,0:T(8,128)} collective-permute-done((f32[16,8,1024]{2,1,0:T(8,128)}, f32[16,8,1024]{2,1,0:T(8,128)}, u32[]{:S(2)}, u32[]{:S(2)}) %collective-permute-start.2) | collective-permute-done | bytes 524320 | tf_op jit(solution)/shard_map/ppermute | solution.py:191
  103.9 1.8 collective-permute-start.7
  106.8 1.6 collective-permute-start.8
  108.4 13.4 %ladder_products.5 = (f32[16,4,1,8,512]{4,3,2,1,0:T(8,128)}, f32[16,4,1,8,512]{4,3,2,1,0:T(8,128)}) custom-call(s32[9]{0:T(128)} %pad_add_fusion.4.bound_ref, s32[3]{0:T(128)} %pad_add_fusion.5.place_ref, f32[32,8,1024]{2,1,0:T(8,128)} %copy-done.5, f32[32,8,1024]{2,1,0:T(8,128)} %collective-permute-done.refs_1_, ...), custom_call_target="tpu_custom_call" | custom-call | flops 6442450944 | bytes 6291456 | tf_op jit(solution)/shard_map/ladder_products/pallas_call | solution.py:138
  121.9 2.3 slice.55
  124.2 7.6 %all-to-all-start.6 = ((f32[32,8,1024]{2,1,0:T(8,128)}), f32[32,8,1024]{2,1,0:T(8,128)}, u32[]{:S(2)}, u32[]{:S(2)}) async-start(f32[32,8,1024]{2,1,0:T(8,128)} %bitcast.13), calls=%async_computation.6 | async-start | bytes 2097152 | tf_op jit(solution)/shard_map/all_to_all | solution.py:187
  132.4 2.4 collective-permute-done.7.refs_3_
  134.8 2.2 collective-permute-done.8.refs_4_
  138.5 1.9 slice.64
  140.8 1.9 slice.65
  142.7 2.8 collective-permute-start.13
  145.5 13.5 %ladder_products.6 = (f32[16,4,1,8,512]{4,3,2,1,0:T(8,128)}, f32[16,4,1,8,512]{4,3,2,1,0:T(8,128)}) custom-call(s32[9]{0:T(128)} %get-tuple-element.99.bound_ref, s32[3]{0:T(128)} %pad_add_fusion.5.place_ref, f32[32,8,1024]{2,1,0:T(8,128)} %copy-done.4, f32[32,8,1024]{2,1,0:T(8,128)} %collective-permute-done.4.refs_1_, ...), custom_call_target="tpu_custom_call" | custom-call | flops 6442450944 | bytes 6291456 | tf_op jit(solution)/shard_map/ladder_products/pallas_call | solution.py:138
  160.3 6.8 %all-to-all-start.3 = ((f32[16,4,1,8,512]{4,3,2,1,0:T(8,128)}), f32[16,4,1,8,512]{4,3,2,1,0:T(8,128)S(1)}, u32[]{:S(2)}, u32[]{:S(2)}) async-start(f32[16,4,1,8,512]{4,3,2,1,0:T(8,128)} %add.83), calls=%async_computation.3 | async-start | bytes 2097152 | tf_op jit(solution)/shard_map/all_to_all | solution.py:242
  167.1 4.9 %collective-permute-done.12.refs_3_ = f32[16,8,1024]{2,1,0:T(8,128)} collective-permute-done((f32[16,8,1024]{2,1,0:T(8,128)}, f32[16,8,1024]{2,1,0:T(8,128)}, u32[]{:S(2)}, u32[]{:S(2)}) %collective-permute-start.12) | collective-permute-done | bytes 524320 | tf_op jit(solution)/shard_map/ppermute | solution.py:191
  172.1 3.2 %collective-permute-start.20 = (f32[32,8,1024]{2,1,0:T(8,128)}, f32[32,8,1024]{2,1,0:T(8,128)}, u32[]{:S(2)}, u32[]{:S(2)}) collective-permute-start(f32[32,8,1024]{2,1,0:T(8,128)} %all-to-all-done.6.refs_0_), channel_id=1, source_target_pairs={{0,96},{32,0},{64,32},{96,64},{1,97},{33,1},{65,33},{97,65},{2,98}... | collective-permute-start | bytes 3145736 | tf_op jit(solution)/shard_map/ppermute | solution.py:191
  175.3 1.9 slice.66
  177.2 1.9 slice.67
  179.1 3.2 %collective-permute-start.18 = (f32[16,8,1024]{2,1,0:T(8,128)}, f32[16,8,1024]{2,1,0:T(8,128)}, u32[]{:S(2)}, u32[]{:S(2)}) collective-permute-start(f32[16,8,1024]{2,1,0:T(8,128)} %slice.67), channel_id=1, source_target_pairs={{0,96},{32,0},{64,32},{96,64},{1,97},{33,1},{65,33},{97,65},{2,98}... | collective-permute-start | bytes 1572872 | tf_op jit(solution)/shard_map/ppermute | solution.py:191
  182.3 13.5 %ladder_products.7 = (f32[16,4,1,8,512]{4,3,2,1,0:T(8,128)}, f32[16,4,1,8,512]{4,3,2,1,0:T(8,128)}) custom-call(s32[9]{0:T(128)} %get-tuple-element.98.bound_ref, s32[3]{0:T(128)} %pad_add_fusion.5.place_ref, f32[32,8,1024]{2,1,0:T(8,128)} %copy-done.3, f32[32,8,1024]{2,1,0:T(8,128)} %collective-permute-done.9.refs_1_, ...), custom_call_target="tpu_custom_call" | custom-call | flops 6442450944 | bytes 6291456 | tf_op jit(solution)/shard_map/ladder_products/pallas_call | solution.py:138
  197.2 6.8 %all-to-all-start.5 = ((f32[16,4,1,8,512]{4,3,2,1,0:T(8,128)}), f32[16,4,1,8,512]{4,3,2,1,0:T(8,128)S(1)}, u32[]{:S(2)}, u32[]{:S(2)}) async-start(f32[16,4,1,8,512]{4,3,2,1,0:T(8,128)} %add.85), calls=%async_computation.5 | async-start | bytes 2097152 | tf_op jit(solution)/shard_map/all_to_all | solution.py:242
  204.6 3.8 %collective-permute-done.17.refs_3_ = f32[16,8,1024]{2,1,0:T(8,128)} collective-permute-done((f32[16,8,1024]{2,1,0:T(8,128)}, f32[16,8,1024]{2,1,0:T(8,128)}, u32[]{:S(2)}, u32[]{:S(2)}) %collective-permute-start.17) | collective-permute-done | bytes 524320 | tf_op jit(solution)/shard_map/ppermute | solution.py:191
  209.8 1.9 slice.69
  211.7 3.2 %collective-permute-start.22 = (f32[16,8,1024]{2,1,0:T(8,128)}, f32[16,8,1024]{2,1,0:T(8,128)}, u32[]{:S(2)}, u32[]{:S(2)}) collective-permute-start(f32[16,8,1024]{2,1,0:T(8,128)} %slice.69), channel_id=1, source_target_pairs={{0,96},{32,0},{64,32},{96,64},{1,97},{33,1},{65,33},{97,65},{2,98}... | collective-permute-start | bytes 1572872 | tf_op jit(solution)/shard_map/ppermute | solution.py:191
  214.9 13.5 %ladder_products.8 = (f32[16,4,1,8,512]{4,3,2,1,0:T(8,128)}, f32[16,4,1,8,512]{4,3,2,1,0:T(8,128)}) custom-call(s32[9]{0:T(128)} %get-tuple-element.97.bound_ref, s32[3]{0:T(128)} %pad_add_fusion.5.place_ref, f32[32,8,1024]{2,1,0:T(8,128)} %all-to-all-done.4.refs_0_, f32[32,8,1024]{2,1,0:T(8,128)} %collective-permute-done.14.refs_1_, ...), custom_call_target="tpu_custom_call" | custom-call | flops 6442450944 | bytes 6291456 | tf_op jit(solution)/shard_map/ladder_products/pallas_call | solution.py:138
  228.6 2.4 add.87
  230.9 6.7 %all-to-all-start.7 = ((f32[16,4,1,8,512]{4,3,2,1,0:T(8,128)}), f32[16,4,1,8,512]{4,3,2,1,0:T(8,128)S(1)}, u32[]{:S(2)}, u32[]{:S(2)}) async-start(f32[16,4,1,8,512]{4,3,2,1,0:T(8,128)} %add.87), calls=%async_computation.7 | async-start | bytes 2097152 | tf_op jit(solution)/shard_map/all_to_all | solution.py:242
  237.6 13.4 %ladder_products.9 = (f32[16,4,1,8,512]{4,3,2,1,0:T(8,128)}, f32[16,4,1,8,512]{4,3,2,1,0:T(8,128)}) custom-call(s32[9]{0:T(128)} %get-tuple-element.96.bound_ref, s32[3]{0:T(128)} %pad_add_fusion.5.place_ref, f32[32,8,1024]{2,1,0:T(8,128)} %all-to-all-done.6.refs_0_, f32[32,8,1024]{2,1,0:T(8,128)} %collective-permute-done.19.refs_1_, ...), custom_call_target="tpu_custom_call" | custom-call | flops 6442450944 | bytes 6291456 | tf_op jit(solution)/shard_map/ladder_products/pallas_call | solution.py:138
  251.4 2.8 add.89
  254.2 1.9 all-to-all-done.7
  256.1 5.2 %all-to-all-start.8 = ((f32[16,4,1,8,512]{4,3,2,1,0:T(8,128)}), f32[16,4,1,8,512]{4,3,2,1,0:T(8,128)}, u32[]{:S(2)}, u32[]{:S(2)}) async-start(f32[16,4,1,8,512]{4,3,2,1,0:T(8,128)} %add.89), calls=%async_computation.8 | async-start | bytes 2097152 | tf_op jit(solution)/shard_map/all_to_all | solution.py:242
  262.5 2.8 add.91
  265.2 14.5 %all-to-all-done.8 = f32[16,4,1,8,512]{4,3,2,1,0:T(8,128)} async-done(((f32[16,4,1,8,512]{4,3,2,1,0:T(8,128)}), f32[16,4,1,8,512]{4,3,2,1,0:T(8,128)}, u32[]{:S(2)}, u32[]{:S(2)}) %all-to-all-start.8) | async-done | bytes 1048608 | tf_op jit(solution)/shard_map/all_to_all | solution.py:242
  279.8 4.3 %all-to-all-start.9 = ((f32[16,4,1,8,512]{4,3,2,1,0:T(8,128)}), f32[16,4,1,8,512]{4,3,2,1,0:T(8,128)}, u32[]{:S(2)}, u32[]{:S(2)}) async-start(f32[16,4,1,8,512]{4,3,2,1,0:T(8,128)} %add.91), calls=%async_computation.9 | async-start | bytes 2097152 | tf_op jit(solution)/shard_map/all_to_all | solution.py:242
  285.7 14.6 %all-to-all-done.9 = f32[16,4,1,8,512]{4,3,2,1,0:T(8,128)} async-done(((f32[16,4,1,8,512]{4,3,2,1,0:T(8,128)}), f32[16,4,1,8,512]{4,3,2,1,0:T(8,128)}, u32[]{:S(2)}, u32[]{:S(2)}) %all-to-all-start.9) | async-done | bytes 1048608 | tf_op jit(solution)/shard_map/all_to_all | solution.py:242
  (95 shorter events, 20.8 us)
Async XLA Ops:
  0.0 36.4 %copy-start.8 = (s32[8]{0:T(128)S(1)}, s32[8]{0:T(128)}, u32[]{:S(2)}) copy-start(s32[8]{0:T(128)} %param.11) | copy-start | bytes 100
  26.3 26.7 %copy-start.5 = (f32[32,8,1024]{2,1,0:T(8,128)}, f32[32,8,1024]{2,1,0:T(8,128)S(1)}, u32[]{:S(2)}) copy-start(f32[32,8,1024]{2,1,0:T(8,128)S(1)} %all_to_all.50.refs_0_) | copy-start | bytes 3145732
  29.0 24.1 %all-to-all-start.1 = ((f32[32,8,1024]{2,1,0:T(8,128)}), f32[32,8,1024]{2,1,0:T(8,128)S(1)}, u32[]{:S(2)}, u32[]{:S(2)}) async-start(f32[32,8,1024]{2,1,0:T(8,128)} %bitcast.5), calls=%async_computation.1 | async-start | bytes 2097152 | tf_op jit(solution)/shard_map/all_to_all | solution.py:187
  33.0 33.5 %collective-permute-start = (f32[32,8,1024]{2,1,0:T(8,128)S(1)}, f32[32,8,1024]{2,1,0:T(8,128)}, u32[]{:S(2)}, u32[]{:S(2)}) collective-permute-start(f32[32,8,1024]{2,1,0:T(8,128)S(1)} %all_to_all.50.refs_0_), channel_id=1, source_target_pairs={{0,32},{32,64},{64,96},{96,0},{1,33},{33,65},{65,97},{97,1},{2,34}... | collective-permute-start | bytes 3145736 | tf_op jit(solution)/shard_map/ppermute | solution.py:191
  34.6 33.9 %collective-permute-start.1 = (f32[32,8,1024]{2,1,0:T(8,128)S(1)}, f32[32,8,1024]{2,1,0:T(8,128)}, u32[]{:S(2)}, u32[]{:S(2)}) collective-permute-start(f32[32,8,1024]{2,1,0:T(8,128)S(1)} %all_to_all.50.refs_0_), channel_id=1, source_target_pairs={{0,96},{32,0},{64,32},{96,64},{1,97},{33,1},{65,33},{97,65},{2,98}... | collective-permute-start | bytes 3145736 | tf_op jit(solution)/shard_map/ppermute | solution.py:191
  36.9 29.5 %copy-start.10 = (s32[8]{0:T(128)S(1)}, s32[8]{0:T(128)}, u32[]{:S(2)}) copy-start(s32[8]{0:T(128)} %param.10) | copy-start | bytes 100
  53.1 29.5 %copy-start.4 = (f32[32,8,1024]{2,1,0:T(8,128)}, f32[32,8,1024]{2,1,0:T(8,128)S(1)}, u32[]{:S(2)}) copy-start(f32[32,8,1024]{2,1,0:T(8,128)S(1)} %all-to-all-done.1.refs_0_) | copy-start | bytes 3145732
  55.7 24.2 %all-to-all-start.2 = ((f32[32,8,1024]{2,1,0:T(8,128)}), f32[32,8,1024]{2,1,0:T(8,128)S(1)}, u32[]{:S(2)}, u32[]{:S(2)}) async-start(f32[32,8,1024]{2,1,0:T(8,128)} %bitcast.7), calls=%async_computation.2 | async-start | bytes 2097152 | tf_op jit(solution)/shard_map/all_to_all | solution.py:187
  63.1 39.0 %collective-permute-start.4 = (f32[32,8,1024]{2,1,0:T(8,128)S(1)}, f32[32,8,1024]{2,1,0:T(8,128)}, u32[]{:S(2)}, u32[]{:S(2)}) collective-permute-start(f32[32,8,1024]{2,1,0:T(8,128)S(1)} %all-to-all-done.1.refs_0_), channel_id=1, source_target_pairs={{0,32},{32,64},{64,96},{96,0},{1,33},{33,65},{65,97},{97,1},{2,34}... | collective-permute-start | bytes 3145736 | tf_op jit(solution)/shard_map/ppermute | solution.py:191
  63.4 39.4 %collective-permute-start.5 = (f32[32,8,1024]{2,1,0:T(8,128)S(1)}, f32[32,8,1024]{2,1,0:T(8,128)}, u32[]{:S(2)}, u32[]{:S(2)}) collective-permute-start(f32[32,8,1024]{2,1,0:T(8,128)S(1)} %all-to-all-done.1.refs_0_), channel_id=1, source_target_pairs={{0,96},{32,0},{64,32},{96,64},{1,97},{33,1},{65,33},{97,65},{2,98}... | collective-permute-start | bytes 3145736 | tf_op jit(solution)/shard_map/ppermute | solution.py:191
  68.5 33.2 %collective-permute-start.2 = (f32[16,8,1024]{2,1,0:T(8,128)}, f32[16,8,1024]{2,1,0:T(8,128)}, u32[]{:S(2)}, u32[]{:S(2)}) collective-permute-start(f32[16,8,1024]{2,1,0:T(8,128)} %slice.60), channel_id=1, source_target_pairs={{0,32},{32,64},{64,96},{96,0},{1,33},{33,65},{65,97},{97,1},{2,34}... | collective-permute-start | bytes 1572872 | tf_op jit(solution)/shard_map/ppermute | solution.py:191
  69.6 32.5 %collective-permute-start.3 = (f32[16,8,1024]{2,1,0:T(8,128)S(1)}, f32[16,8,1024]{2,1,0:T(8,128)S(1)}, u32[]{:S(2)}, u32[]{:S(2)}) collective-permute-start(f32[16,8,1024]{2,1,0:T(8,128)S(1)} %slice.61), channel_id=1, source_target_pairs={{0,96},{32,0},{64,32},{96,64},{1,97},{33,1},{65,33},{97,65},{2,98}... | collective-permute-start | bytes 1572872 | tf_op jit(solution)/shard_map/ppermute | solution.py:191
  79.9 41.9 %copy-start.3 = (f32[32,8,1024]{2,1,0:T(8,128)}, f32[32,8,1024]{2,1,0:T(8,128)S(1)}, u32[]{:S(2)}) copy-start(f32[32,8,1024]{2,1,0:T(8,128)S(1)} %all-to-all-done.2.refs_0_) | copy-start | bytes 3145732
  82.6 39.3 %all-to-all-start.4 = ((f32[32,8,1024]{2,1,0:T(8,128)}), f32[32,8,1024]{2,1,0:T(8,128)}, u32[]{:S(2)}, u32[]{:S(2)}) async-start(f32[32,8,1024]{2,1,0:T(8,128)} %bitcast.10), calls=%async_computation.4 | async-start | bytes 2097152 | tf_op jit(solution)/shard_map/all_to_all | solution.py:187
  88.4 50.0 %collective-permute-start.9 = (f32[32,8,1024]{2,1,0:T(8,128)S(1)}, f32[32,8,1024]{2,1,0:T(8,128)}, u32[]{:S(2)}, u32[]{:S(2)}) collective-permute-start(f32[32,8,1024]{2,1,0:T(8,128)S(1)} %all-to-all-done.2.refs_0_), channel_id=1, source_target_pairs={{0,32},{32,64},{64,96},{96,0},{1,33},{33,65},{65,97},{97,1},{2,34}... | collective-permute-start | bytes 3145736 | tf_op jit(solution)/shard_map/ppermute | solution.py:191
  101.7 36.8 %collective-permute-start.10 = (f32[32,8,1024]{2,1,0:T(8,128)S(1)}, f32[32,8,1024]{2,1,0:T(8,128)}, u32[]{:S(2)}, u32[]{:S(2)}) collective-permute-start(f32[32,8,1024]{2,1,0:T(8,128)S(1)} %all-to-all-done.2.refs_0_), channel_id=1, source_target_pairs={{0,96},{32,0},{64,32},{96,64},{1,97},{33,1},{65,33},{97,65},{2,98}... | collective-permute-start | bytes 3145736 | tf_op jit(solution)/shard_map/ppermute | solution.py:191
  102.0 0.8 copy-start.9
  103.9 30.8 %collective-permute-start.7 = (f32[16,8,1024]{2,1,0:T(8,128)S(1)}, f32[16,8,1024]{2,1,0:T(8,128)}, u32[]{:S(2)}, u32[]{:S(2)}) collective-permute-start(f32[16,8,1024]{2,1,0:T(8,128)S(1)} %slice.62), channel_id=1, source_target_pairs={{0,32},{32,64},{64,96},{96,0},{1,33},{33,65},{65,97},{97,1},{2,34}... | collective-permute-start | bytes 1572872 | tf_op jit(solution)/shard_map/ppermute | solution.py:191
  106.8 30.2 %collective-permute-start.8 = (f32[16,8,1024]{2,1,0:T(8,128)S(1)}, f32[16,8,1024]{2,1,0:T(8,128)}, u32[]{:S(2)}, u32[]{:S(2)}) collective-permute-start(f32[16,8,1024]{2,1,0:T(8,128)S(1)} %slice.63), channel_id=1, source_target_pairs={{0,96},{32,0},{64,32},{96,64},{1,97},{33,1},{65,33},{97,65},{2,98}... | collective-permute-start | bytes 1572872 | tf_op jit(solution)/shard_map/ppermute | solution.py:191
  121.8 37.2 %collective-permute-start.6 = (f32[16,4,1,8,512]{4,3,2,1,0:T(8,128)}, f32[16,4,1,8,512]{4,3,2,1,0:T(8,128)S(1)}, u32[]{:S(2)}, u32[]{:S(2)}) collective-permute-start(f32[16,4,1,8,512]{4,3,2,1,0:T(8,128)} %get-tuple-element.57), channel_id=1, source_target_pairs={{0,1},{1,0},{2,3},{3,2},{4,5},{5,4},{6,7},{7,6},{8,9},{9,8},{10,11... | collective-permute-start | bytes 3145736 | tf_op jit(solution)/shard_map/ppermute | solution.py:238
  124.2 36.1 %all-to-all-start.6 = ((f32[32,8,1024]{2,1,0:T(8,128)}), f32[32,8,1024]{2,1,0:T(8,128)}, u32[]{:S(2)}, u32[]{:S(2)}) async-start(f32[32,8,1024]{2,1,0:T(8,128)} %bitcast.13), calls=%async_computation.6 | async-start | bytes 2097152 | tf_op jit(solution)/shard_map/all_to_all | solution.py:187
  134.8 40.5 %collective-permute-start.14 = (f32[32,8,1024]{2,1,0:T(8,128)}, f32[32,8,1024]{2,1,0:T(8,128)}, u32[]{:S(2)}, u32[]{:S(2)}) collective-permute-start(f32[32,8,1024]{2,1,0:T(8,128)} %all-to-all-done.4.refs_0_), channel_id=1, source_target_pairs={{0,32},{32,64},{64,96},{96,0},{1,33},{33,65},{65,97},{97,1},{2,34}... | collective-permute-start | bytes 3145736 | tf_op jit(solution)/shard_map/ppermute | solution.py:191
  136.9 38.4 %collective-permute-start.15 = (f32[32,8,1024]{2,1,0:T(8,128)}, f32[32,8,1024]{2,1,0:T(8,128)}, u32[]{:S(2)}, u32[]{:S(2)}) collective-permute-start(f32[32,8,1024]{2,1,0:T(8,128)} %all-to-all-done.4.refs_0_), channel_id=1, source_target_pairs={{0,96},{32,0},{64,32},{96,64},{1,97},{33,1},{65,33},{97,65},{2,98}... | collective-permute-start | bytes 3145736 | tf_op jit(solution)/shard_map/ppermute | solution.py:191
  140.4 31.7 %collective-permute-start.12 = (f32[16,8,1024]{2,1,0:T(8,128)}, f32[16,8,1024]{2,1,0:T(8,128)}, u32[]{:S(2)}, u32[]{:S(2)}) collective-permute-start(f32[16,8,1024]{2,1,0:T(8,128)} %slice.64), channel_id=1, source_target_pairs={{0,32},{32,64},{64,96},{96,0},{1,33},{33,65},{65,97},{97,1},{2,34}... | collective-permute-start | bytes 1572872 | tf_op jit(solution)/shard_map/ppermute | solution.py:191
  142.7 29.3 %collective-permute-start.13 = (f32[16,8,1024]{2,1,0:T(8,128)}, f32[16,8,1024]{2,1,0:T(8,128)}, u32[]{:S(2)}, u32[]{:S(2)}) collective-permute-start(f32[16,8,1024]{2,1,0:T(8,128)} %slice.65), channel_id=1, source_target_pairs={{0,96},{32,0},{64,32},{96,64},{1,97},{33,1},{65,33},{97,65},{2,98}... | collective-permute-start | bytes 1572872 | tf_op jit(solution)/shard_map/ppermute | solution.py:191
  145.5 13.6 %copy-start.2 = (f32[16,4,1,8,512]{4,3,2,1,0:T(8,128)S(1)}, f32[16,4,1,8,512]{4,3,2,1,0:T(8,128)}, u32[]{:S(2)}) copy-start(f32[16,4,1,8,512]{4,3,2,1,0:T(8,128)} %get-tuple-element.56) | copy-start | bytes 3145732
  159.0 36.9 %collective-permute-start.11 = (f32[16,4,1,8,512]{4,3,2,1,0:T(8,128)}, f32[16,4,1,8,512]{4,3,2,1,0:T(8,128)S(1)}, u32[]{:S(2)}, u32[]{:S(2)}) collective-permute-start(f32[16,4,1,8,512]{4,3,2,1,0:T(8,128)} %get-tuple-element.65), channel_id=1, source_target_pairs={{0,1},{1,0},{2,3},{3,2},{4,5},{5,4},{6,7},{7,6},{8,9},{9,8},{10,11... | collective-permute-start | bytes 3145736 | tf_op jit(solution)/shard_map/ppermute | solution.py:238
  160.3 36.9 %all-to-all-start.3 = ((f32[16,4,1,8,512]{4,3,2,1,0:T(8,128)}), f32[16,4,1,8,512]{4,3,2,1,0:T(8,128)S(1)}, u32[]{:S(2)}, u32[]{:S(2)}) async-start(f32[16,4,1,8,512]{4,3,2,1,0:T(8,128)} %add.83), calls=%async_computation.3 | async-start | bytes 2097152 | tf_op jit(solution)/shard_map/all_to_all | solution.py:242
  172.1 36.4 %collective-permute-start.19 = (f32[32,8,1024]{2,1,0:T(8,128)}, f32[32,8,1024]{2,1,0:T(8,128)}, u32[]{:S(2)}, u32[]{:S(2)}) collective-permute-start(f32[32,8,1024]{2,1,0:T(8,128)} %all-to-all-done.6.refs_0_), channel_id=1, source_target_pairs={{0,32},{32,64},{64,96},{96,0},{1,33},{33,65},{65,97},{97,1},{2,34}... | collective-permute-start | bytes 3145736 | tf_op jit(solution)/shard_map/ppermute | solution.py:191
  172.1 36.4 %collective-permute-start.20 = (f32[32,8,1024]{2,1,0:T(8,128)}, f32[32,8,1024]{2,1,0:T(8,128)}, u32[]{:S(2)}, u32[]{:S(2)}) collective-permute-start(f32[32,8,1024]{2,1,0:T(8,128)} %all-to-all-done.6.refs_0_), channel_id=1, source_target_pairs={{0,96},{32,0},{64,32},{96,64},{1,97},{33,1},{65,33},{97,65},{2,98}... | collective-permute-start | bytes 3145736 | tf_op jit(solution)/shard_map/ppermute | solution.py:191
  177.2 31.2 %collective-permute-start.17 = (f32[16,8,1024]{2,1,0:T(8,128)}, f32[16,8,1024]{2,1,0:T(8,128)}, u32[]{:S(2)}, u32[]{:S(2)}) collective-permute-start(f32[16,8,1024]{2,1,0:T(8,128)} %slice.66), channel_id=1, source_target_pairs={{0,32},{32,64},{64,96},{96,0},{1,33},{33,65},{65,97},{97,1},{2,34}... | collective-permute-start | bytes 1572872 | tf_op jit(solution)/shard_map/ppermute | solution.py:191
  179.1 29.3 %collective-permute-start.18 = (f32[16,8,1024]{2,1,0:T(8,128)}, f32[16,8,1024]{2,1,0:T(8,128)}, u32[]{:S(2)}, u32[]{:S(2)}) collective-permute-start(f32[16,8,1024]{2,1,0:T(8,128)} %slice.67), channel_id=1, source_target_pairs={{0,96},{32,0},{64,32},{96,64},{1,97},{33,1},{65,33},{97,65},{2,98}... | collective-permute-start | bytes 1572872 | tf_op jit(solution)/shard_map/ppermute | solution.py:191
  182.3 13.6 %copy-start.1 = (f32[16,4,1,8,512]{4,3,2,1,0:T(8,128)S(1)}, f32[16,4,1,8,512]{4,3,2,1,0:T(8,128)}, u32[]{:S(2)}) copy-start(f32[16,4,1,8,512]{4,3,2,1,0:T(8,128)} %get-tuple-element.64) | copy-start | bytes 3145732
  195.9 32.7 %collective-permute-start.16 = (f32[16,4,1,8,512]{4,3,2,1,0:T(8,128)}, f32[16,4,1,8,512]{4,3,2,1,0:T(8,128)}, u32[]{:S(2)}, u32[]{:S(2)}) collective-permute-start(f32[16,4,1,8,512]{4,3,2,1,0:T(8,128)} %get-tuple-element.73), channel_id=1, source_target_pairs={{0,1},{1,0},{2,3},{3,2},{4,5},{5,4},{6,7},{7,6},{8,9},{9,8},{10,11... | collective-permute-start | bytes 3145736 | tf_op jit(solution)/shard_map/ppermute | solution.py:238
  197.2 33.8 %all-to-all-start.5 = ((f32[16,4,1,8,512]{4,3,2,1,0:T(8,128)}), f32[16,4,1,8,512]{4,3,2,1,0:T(8,128)S(1)}, u32[]{:S(2)}, u32[]{:S(2)}) async-start(f32[16,4,1,8,512]{4,3,2,1,0:T(8,128)} %add.85), calls=%async_computation.5 | async-start | bytes 2097152 | tf_op jit(solution)/shard_map/all_to_all | solution.py:242
  209.5 18.9 %collective-permute-start.21 = (f32[16,8,1024]{2,1,0:T(8,128)S(1)}, f32[16,8,1024]{2,1,0:T(8,128)}, u32[]{:S(2)}, u32[]{:S(2)}) collective-permute-start(f32[16,8,1024]{2,1,0:T(8,128)S(1)} %slice.68), channel_id=1, source_target_pairs={{0,32},{32,64},{64,96},{96,0},{1,33},{33,65},{65,97},{97,1},{2,34}... | collective-permute-start | bytes 1572872 | tf_op jit(solution)/shard_map/ppermute | solution.py:191
  211.7 16.8 %collective-permute-start.22 = (f32[16,8,1024]{2,1,0:T(8,128)}, f32[16,8,1024]{2,1,0:T(8,128)}, u32[]{:S(2)}, u32[]{:S(2)}) collective-permute-start(f32[16,8,1024]{2,1,0:T(8,128)} %slice.69), channel_id=1, source_target_pairs={{0,96},{32,0},{64,32},{96,64},{1,97},{33,1},{65,33},{97,65},{2,98}... | collective-permute-start | bytes 1572872 | tf_op jit(solution)/shard_map/ppermute | solution.py:191
  214.9 13.7 %copy-start = (f32[16,4,1,8,512]{4,3,2,1,0:T(8,128)S(1)}, f32[16,4,1,8,512]{4,3,2,1,0:T(8,128)}, u32[]{:S(2)}) copy-start(f32[16,4,1,8,512]{4,3,2,1,0:T(8,128)} %get-tuple-element.72) | copy-start | bytes 3145732
  228.5 22.9 %collective-permute-start.23 = (f32[16,4,1,8,512]{4,3,2,1,0:T(8,128)}, f32[16,4,1,8,512]{4,3,2,1,0:T(8,128)}, u32[]{:S(2)}, u32[]{:S(2)}) collective-permute-start(f32[16,4,1,8,512]{4,3,2,1,0:T(8,128)} %get-tuple-element.81), channel_id=1, source_target_pairs={{0,1},{1,0},{2,3},{3,2},{4,5},{5,4},{6,7},{7,6},{8,9},{9,8},{10,11... | collective-permute-start | bytes 3145736 | tf_op jit(solution)/shard_map/ppermute | solution.py:238
  230.9 25.1 %all-to-all-start.7 = ((f32[16,4,1,8,512]{4,3,2,1,0:T(8,128)}), f32[16,4,1,8,512]{4,3,2,1,0:T(8,128)S(1)}, u32[]{:S(2)}, u32[]{:S(2)}) async-start(f32[16,4,1,8,512]{4,3,2,1,0:T(8,128)} %add.87), calls=%async_computation.7 | async-start | bytes 2097152 | tf_op jit(solution)/shard_map/all_to_all | solution.py:242
  251.1 10.5 %copy-start.6 = (f32[8,512]{1,0:T(8,128)S(1)}, f32[8,512]{1,0:T(8,128)}, u32[]{:S(2)}) copy-start(f32[8,512]{1,0:T(8,128)} %param.9) | copy-start | bytes 49156
  251.1 11.4 %collective-permute-start.24 = (f32[16,4,1,8,512]{4,3,2,1,0:T(8,128)}, f32[16,4,1,8,512]{4,3,2,1,0:T(8,128)}, u32[]{:S(2)}, u32[]{:S(2)}) collective-permute-start(f32[16,4,1,8,512]{4,3,2,1,0:T(8,128)} %get-tuple-element.88), channel_id=1, source_target_pairs={{0,1},{1,0},{2,3},{3,2},{4,5},{5,4},{6,7},{7,6},{8,9},{9,8},{10,11... | collective-permute-start | bytes 3145736 | tf_op jit(solution)/shard_map/ppermute | solution.py:238
  256.1 23.7 %all-to-all-start.8 = ((f32[16,4,1,8,512]{4,3,2,1,0:T(8,128)}), f32[16,4,1,8,512]{4,3,2,1,0:T(8,128)}, u32[]{:S(2)}, u32[]{:S(2)}) async-start(f32[16,4,1,8,512]{4,3,2,1,0:T(8,128)} %add.89), calls=%async_computation.8 | async-start | bytes 2097152 | tf_op jit(solution)/shard_map/all_to_all | solution.py:242
  262.5 39.2 %copy-start.7 = (f32[160]{0:T(256)S(1)}, f32[160]{0:T(256)}, u32[]{:S(2)}) copy-start(f32[160]{0:T(256)} %param.8) | copy-start | bytes 1924
  279.8 20.6 %all-to-all-start.9 = ((f32[16,4,1,8,512]{4,3,2,1,0:T(8,128)}), f32[16,4,1,8,512]{4,3,2,1,0:T(8,128)}, u32[]{:S(2)}, u32[]{:S(2)}) async-start(f32[16,4,1,8,512]{4,3,2,1,0:T(8,128)} %add.91), calls=%async_computation.9 | async-start | bytes 2097152 | tf_op jit(solution)/shard_map/all_to_all | solution.py:242

commit v4 on v3

--- a/solution.py
+++ b/solution.py
@@ -11,7 +11,7 @@
 TILE = 128
 CORES = 2
 UNITS = (1, 1, 1, 1, 1)
-AHEAD = 2
+AHEAD = 3
 EARLY = 2
 JOINS = (1, 2, 3, 4, 5)
 DIRECT = False

time: 304 us -> 305 us (level)
  no operation moved by 1% of the time
where the time goes in v4:
time: 305 us; the launch traced here: 303 us
  Pallas kernels  84.1 us (28%)
  starting transfers between devices  82.9 us (27%)
  waiting for transfers between devices  63.9 us (21%)
  local copies, waits for them, and re-layouts  28.2 us (9%)
  blocking collectives  25 us (8%)
  other arithmetic  18.1 us (6%)
    pallas_call x5, Pallas kernels, products(): pl.pallas_call(functools.partial(product_kernel, steps=steps), in_specs=[...  67.9 us
    all_to_all x5, waiting for transfers between devices, body(): lax.all_to_all(group[0], ('col', 'deep'), split_axis=0, concat_axis=0, ti...  30.9 us
    all_to_all x5, starting transfers between devices, body(): lax.all_to_all(group[0], ('col', 'deep'), split_axis=0, concat_axis=0, ti...  29.9 us
    all_to_all x1, blocking collectives, body(): lax.all_to_all(own, ('col', 'deep', 'core'), split_axis=0, concat_axis=0,...  25 us
    ppermute x10, starting transfers between devices, pair(): lax.ppermute(right, 'row', ring(rows_x, rows_x - 1))  24 us
    ppermute x10, waiting for transfers between devices, pair(): lax.ppermute(left, 'row', ring(rows_x, 1))  23.7 us
    all_to_all x4, starting transfers between devices, body(): lax.all_to_all(own, ('col', 'deep', 'core'), split_axis=0, concat_axis=0,...  23.7 us
    pallas_call x1, Pallas kernels, split_ladder(): pl.pallas_call(split_kernel, grid_spec=pltpu.PrefetchScalarGridSpec(num_s...  16.2 us
  transfers between devices with their start and end apart: 34, of which 9 were waited for; matrix products, arithmetic and copies ran while one was open for 13% of the time, Pallas kernels for 28%

profile of v4, /device:TPU:0, one launch (start us, length us, event | category | flops | bytes accessed | tf_op | source)
XLA Modules:
  0.0 302.8 jit_solution(14753019786120694986)
XLA Ops:
  1.3 25.0 %all_to_all.50.refs_0_ = f32[32,8,1024]{2,1,0:T(8,128)S(1)} all-to-all(f32[32,8,1024]{2,1,0:T(8,128)S(1)} %bitcast.31), channel_id=1, replica_groups=mesh['row'=4,'col'=4,'deep'=4,'core'=2] {'col','deep','core'}, dimensions={0} | all-to-all | bytes 2097152 | tf_op jit(solution)/shard_map/all_to_all | solution.py:187
  26.3 2.6 slice.48
  29.0 4.1 %all-to-all-start.1 = ((f32[32,8,1024]{2,1,0:T(8,128)}), f32[32,8,1024]{2,1,0:T(8,128)S(1)}, u32[]{:S(2)}, u32[]{:S(2)}) async-start(f32[32,8,1024]{2,1,0:T(8,128)} %bitcast.5), calls=%async_computation.1 | async-start | bytes 2097152 | tf_op jit(solution)/shard_map/all_to_all | solution.py:187
  33.0 1.6 collective-permute-start
  34.6 1.7 collective-permute-start.1
  36.9 16.2 %split_ladder.1 = (bf16[8,1024,512]{2,1,0:T(8,128)(2,1)}, bf16[8,1024,512]{2,1,0:T(8,128)(2,1)}) custom-call(s32[8]{0:T(128)} %broadcast_subtract_fusion.count_ref, f32[8,512,1024]{2,1,0:T(8,128)} %ladder_ref.1), custom_call_target="tpu_custom_call" | custom-call | flops 33554432 | bytes 16777216 | tf_op jit(solution)/shard_map/split_ladder/pallas_call | solution.py:41
  53.1 2.6 slice.49
  55.7 7.4 %all-to-all-start.2 = ((f32[32,8,1024]{2,1,0:T(8,128)}), f32[32,8,1024]{2,1,0:T(8,128)S(1)}, u32[]{:S(2)}, u32[]{:S(2)}) async-start(f32[32,8,1024]{2,1,0:T(8,128)} %bitcast.7), calls=%async_computation.2 | async-start | bytes 2097152 | tf_op jit(solution)/shard_map/all_to_all | solution.py:187
  63.4 3.0 collective-permute-start.5
  66.5 1.9 slice.60
  69.6 3.3 %collective-permute-start.3 = (f32[16,8,1024]{2,1,0:T(8,128)S(1)}, f32[16,8,1024]{2,1,0:T(8,128)S(1)}, u32[]{:S(2)}, u32[]{:S(2)}) collective-permute-start(f32[16,8,1024]{2,1,0:T(8,128)S(1)} %slice.61), channel_id=1, source_target_pairs={{0,96},{32,0},{64,32},{96,64},{1,97},{33,1},{65,33},{97,65},{2,98}... | collective-permute-start | bytes 1572872 | tf_op jit(solution)/shard_map/ppermute | solution.py:191
  72.9 7.0 %all-to-all-done.2.refs_0_ = f32[32,8,1024]{2,1,0:T(8,128)S(1)} async-done(((f32[32,8,1024]{2,1,0:T(8,128)}), f32[32,8,1024]{2,1,0:T(8,128)S(1)}, u32[]{:S(2)}, u32[]{:S(2)}) %all-to-all-start.2) | async-done | bytes 1048608 | tf_op jit(solution)/shard_map/all_to_all | solution.py:187
  79.9 2.6 slice.52
  82.6 4.7 %all-to-all-start.4 = ((f32[32,8,1024]{2,1,0:T(8,128)}), f32[32,8,1024]{2,1,0:T(8,128)}, u32[]{:S(2)}, u32[]{:S(2)}) async-start(f32[32,8,1024]{2,1,0:T(8,128)} %bitcast.10), calls=%async_computation.4 | async-start | bytes 2097152 | tf_op jit(solution)/shard_map/all_to_all | solution.py:187
  88.7 13.0 %collective-permute-done.2.refs_3_ = f32[16,8,1024]{2,1,0:T(8,128)} collective-permute-done((f32[16,8,1024]{2,1,0:T(8,128)}, f32[16,8,1024]{2,1,0:T(8,128)}, u32[]{:S(2)}, u32[]{:S(2)}) %collective-permute-start.2) | collective-permute-done | bytes 524320 | tf_op jit(solution)/shard_map/ppermute | solution.py:191
  103.9 1.8 collective-permute-start.7
  106.8 1.6 collective-permute-start.8
  108.4 13.5 %ladder_products.5 = (f32[16,4,1,8,512]{4,3,2,1,0:T(8,128)}, f32[16,4,1,8,512]{4,3,2,1,0:T(8,128)}) custom-call(s32[9]{0:T(128)} %pad_add_fusion.4.bound_ref, s32[3]{0:T(128)} %pad_add_fusion.5.place_ref, f32[32,8,1024]{2,1,0:T(8,128)} %copy-done.5, f32[32,8,1024]{2,1,0:T(8,128)} %collective-permute-done.refs_1_, ...), custom_call_target="tpu_custom_call" | custom-call | flops 6442450944 | bytes 6291456 | tf_op jit(solution)/shard_map/ladder_products/pallas_call | solution.py:138
  122.0 2.3 slice.55
  124.3 7.6 %all-to-all-start.6 = ((f32[32,8,1024]{2,1,0:T(8,128)}), f32[32,8,1024]{2,1,0:T(8,128)}, u32[]{:S(2)}, u32[]{:S(2)}) async-start(f32[32,8,1024]{2,1,0:T(8,128)} %bitcast.13), calls=%async_computation.6 | async-start | bytes 2097152 | tf_op jit(solution)/shard_map/all_to_all | solution.py:187
  132.5 2.3 collective-permute-done.7.refs_3_
  134.8 2.2 collective-permute-done.8.refs_4_
  138.5 1.9 slice.64
  140.8 1.9 slice.65
  142.7 2.8 collective-permute-start.13
  145.5 13.6 %ladder_products.6 = (f32[16,4,1,8,512]{4,3,2,1,0:T(8,128)}, f32[16,4,1,8,512]{4,3,2,1,0:T(8,128)}) custom-call(s32[9]{0:T(128)} %get-tuple-element.99.bound_ref, s32[3]{0:T(128)} %pad_add_fusion.5.place_ref, f32[32,8,1024]{2,1,0:T(8,128)} %copy-done.4, f32[32,8,1024]{2,1,0:T(8,128)} %collective-permute-done.4.refs_1_, ...), custom_call_target="tpu_custom_call" | custom-call | flops 6442450944 | bytes 6291456 | tf_op jit(solution)/shard_map/ladder_products/pallas_call | solution.py:138
  160.4 6.8 %all-to-all-start.3 = ((f32[16,4,1,8,512]{4,3,2,1,0:T(8,128)}), f32[16,4,1,8,512]{4,3,2,1,0:T(8,128)S(1)}, u32[]{:S(2)}, u32[]{:S(2)}) async-start(f32[16,4,1,8,512]{4,3,2,1,0:T(8,128)} %add.83), calls=%async_computation.3 | async-start | bytes 2097152 | tf_op jit(solution)/shard_map/all_to_all | solution.py:242
  167.2 4.8 %collective-permute-done.12.refs_3_ = f32[16,8,1024]{2,1,0:T(8,128)} collective-permute-done((f32[16,8,1024]{2,1,0:T(8,128)}, f32[16,8,1024]{2,1,0:T(8,128)}, u32[]{:S(2)}, u32[]{:S(2)}) %collective-permute-start.12) | collective-permute-done | bytes 524320 | tf_op jit(solution)/shard_map/ppermute | solution.py:191
  172.1 3.2 %collective-permute-start.20 = (f32[32,8,1024]{2,1,0:T(8,128)}, f32[32,8,1024]{2,1,0:T(8,128)}, u32[]{:S(2)}, u32[]{:S(2)}) collective-permute-start(f32[32,8,1024]{2,1,0:T(8,128)} %all-to-all-done.6.refs_0_), channel_id=1, source_target_pairs={{0,96},{32,0},{64,32},{96,64},{1,97},{33,1},{65,33},{97,65},{2,98}... | collective-permute-start | bytes 3145736 | tf_op jit(solution)/shard_map/ppermute | solution.py:191
  175.3 1.9 slice.66
  177.2 1.9 slice.67
  179.1 3.2 %collective-permute-start.18 = (f32[16,8,1024]{2,1,0:T(8,128)}, f32[16,8,1024]{2,1,0:T(8,128)}, u32[]{:S(2)}, u32[]{:S(2)}) collective-permute-start(f32[16,8,1024]{2,1,0:T(8,128)} %slice.67), channel_id=1, source_target_pairs={{0,96},{32,0},{64,32},{96,64},{1,97},{33,1},{65,33},{97,65},{2,98}... | collective-permute-start | bytes 1572872 | tf_op jit(solution)/shard_map/ppermute | solution.py:191
  182.3 13.7 %ladder_products.7 = (f32[16,4,1,8,512]{4,3,2,1,0:T(8,128)}, f32[16,4,1,8,512]{4,3,2,1,0:T(8,128)}) custom-call(s32[9]{0:T(128)} %get-tuple-element.98.bound_ref, s32[3]{0:T(128)} %pad_add_fusion.5.place_ref, f32[32,8,1024]{2,1,0:T(8,128)} %copy-done.3, f32[32,8,1024]{2,1,0:T(8,128)} %collective-permute-done.9.refs_1_, ...), custom_call_target="tpu_custom_call" | custom-call | flops 6442450944 | bytes 6291456 | tf_op jit(solution)/shard_map/ladder_products/pallas_call | solution.py:138
  197.3 6.8 %all-to-all-start.5 = ((f32[16,4,1,8,512]{4,3,2,1,0:T(8,128)}), f32[16,4,1,8,512]{4,3,2,1,0:T(8,128)S(1)}, u32[]{:S(2)}, u32[]{:S(2)}) async-start(f32[16,4,1,8,512]{4,3,2,1,0:T(8,128)} %add.85), calls=%async_computation.5 | async-start | bytes 2097152 | tf_op jit(solution)/shard_map/all_to_all | solution.py:242
  204.7 3.7 %collective-permute-done.17.refs_3_ = f32[16,8,1024]{2,1,0:T(8,128)} collective-permute-done((f32[16,8,1024]{2,1,0:T(8,128)}, f32[16,8,1024]{2,1,0:T(8,128)}, u32[]{:S(2)}, u32[]{:S(2)}) %collective-permute-start.17) | collective-permute-done | bytes 524320 | tf_op jit(solution)/shard_map/ppermute | solution.py:191
  209.8 1.9 slice.69
  211.7 3.2 %collective-permute-start.22 = (f32[16,8,1024]{2,1,0:T(8,128)}, f32[16,8,1024]{2,1,0:T(8,128)}, u32[]{:S(2)}, u32[]{:S(2)}) collective-permute-start(f32[16,8,1024]{2,1,0:T(8,128)} %slice.69), channel_id=1, source_target_pairs={{0,96},{32,0},{64,32},{96,64},{1,97},{33,1},{65,33},{97,65},{2,98}... | collective-permute-start | bytes 1572872 | tf_op jit(solution)/shard_map/ppermute | solution.py:191
  214.9 13.6 %ladder_products.8 = (f32[16,4,1,8,512]{4,3,2,1,0:T(8,128)}, f32[16,4,1,8,512]{4,3,2,1,0:T(8,128)}) custom-call(s32[9]{0:T(128)} %get-tuple-element.97.bound_ref, s32[3]{0:T(128)} %pad_add_fusion.5.place_ref, f32[32,8,1024]{2,1,0:T(8,128)} %all-to-all-done.4.refs_0_, f32[32,8,1024]{2,1,0:T(8,128)} %collective-permute-done.14.refs_1_, ...), custom_call_target="tpu_custom_call" | custom-call | flops 6442450944 | bytes 6291456 | tf_op jit(solution)/shard_map/ladder_products/pallas_call | solution.py:138
  228.7 2.4 add.87
  231.1 6.7 %all-to-all-start.7 = ((f32[16,4,1,8,512]{4,3,2,1,0:T(8,128)}), f32[16,4,1,8,512]{4,3,2,1,0:T(8,128)S(1)}, u32[]{:S(2)}, u32[]{:S(2)}) async-start(f32[16,4,1,8,512]{4,3,2,1,0:T(8,128)} %add.87), calls=%async_computation.7 | async-start | bytes 2097152 | tf_op jit(solution)/shard_map/all_to_all | solution.py:242
  237.8 13.6 %ladder_products.9 = (f32[16,4,1,8,512]{4,3,2,1,0:T(8,128)}, f32[16,4,1,8,512]{4,3,2,1,0:T(8,128)}) custom-call(s32[9]{0:T(128)} %get-tuple-element.96.bound_ref, s32[3]{0:T(128)} %pad_add_fusion.5.place_ref, f32[32,8,1024]{2,1,0:T(8,128)} %all-to-all-done.6.refs_0_, f32[32,8,1024]{2,1,0:T(8,128)} %collective-permute-done.19.refs_1_, ...), custom_call_target="tpu_custom_call" | custom-call | flops 6442450944 | bytes 6291456 | tf_op jit(solution)/shard_map/ladder_products/pallas_call | solution.py:138
  251.6 2.8 add.89
  254.4 1.8 all-to-all-done.7
  256.2 5.3 %all-to-all-start.8 = ((f32[16,4,1,8,512]{4,3,2,1,0:T(8,128)}), f32[16,4,1,8,512]{4,3,2,1,0:T(8,128)}, u32[]{:S(2)}, u32[]{:S(2)}) async-start(f32[16,4,1,8,512]{4,3,2,1,0:T(8,128)} %add.89), calls=%async_computation.8 | async-start | bytes 2097152 | tf_op jit(solution)/shard_map/all_to_all | solution.py:242
  262.7 2.8 add.91
  265.5 14.5 %all-to-all-done.8 = f32[16,4,1,8,512]{4,3,2,1,0:T(8,128)} async-done(((f32[16,4,1,8,512]{4,3,2,1,0:T(8,128)}), f32[16,4,1,8,512]{4,3,2,1,0:T(8,128)}, u32[]{:S(2)}, u32[]{:S(2)}) %all-to-all-start.8) | async-done | bytes 1048608 | tf_op jit(solution)/shard_map/all_to_all | solution.py:242
  280.0 4.3 %all-to-all-start.9 = ((f32[16,4,1,8,512]{4,3,2,1,0:T(8,128)}), f32[16,4,1,8,512]{4,3,2,1,0:T(8,128)}, u32[]{:S(2)}, u32[]{:S(2)}) async-start(f32[16,4,1,8,512]{4,3,2,1,0:T(8,128)} %add.91), calls=%async_computation.9 | async-start | bytes 2097152 | tf_op jit(solution)/shard_map/all_to_all | solution.py:242
  286.0 14.6 %all-to-all-done.9 = f32[16,4,1,8,512]{4,3,2,1,0:T(8,128)} async-done(((f32[16,4,1,8,512]{4,3,2,1,0:T(8,128)}), f32[16,4,1,8,512]{4,3,2,1,0:T(8,128)}, u32[]{:S(2)}, u32[]{:S(2)}) %all-to-all-start.9) | async-done | bytes 1048608 | tf_op jit(solution)/shard_map/all_to_all | solution.py:242
  (95 shorter events, 20.8 us)
Async XLA Ops:
  0.0 36.4 %copy-start.8 = (s32[8]{0:T(128)S(1)}, s32[8]{0:T(128)}, u32[]{:S(2)}) copy-start(s32[8]{0:T(128)} %param.11) | copy-start | bytes 100
  26.3 26.7 %copy-start.5 = (f32[32,8,1024]{2,1,0:T(8,128)}, f32[32,8,1024]{2,1,0:T(8,128)S(1)}, u32[]{:S(2)}) copy-start(f32[32,8,1024]{2,1,0:T(8,128)S(1)} %all_to_all.50.refs_0_) | copy-start | bytes 3145732
  29.0 24.1 %all-to-all-start.1 = ((f32[32,8,1024]{2,1,0:T(8,128)}), f32[32,8,1024]{2,1,0:T(8,128)S(1)}, u32[]{:S(2)}, u32[]{:S(2)}) async-start(f32[32,8,1024]{2,1,0:T(8,128)} %bitcast.5), calls=%async_computation.1 | async-start | bytes 2097152 | tf_op jit(solution)/shard_map/all_to_all | solution.py:187
  33.0 33.5 %collective-permute-start = (f32[32,8,1024]{2,1,0:T(8,128)S(1)}, f32[32,8,1024]{2,1,0:T(8,128)}, u32[]{:S(2)}, u32[]{:S(2)}) collective-permute-start(f32[32,8,1024]{2,1,0:T(8,128)S(1)} %all_to_all.50.refs_0_), channel_id=1, source_target_pairs={{0,32},{32,64},{64,96},{96,0},{1,33},{33,65},{65,97},{97,1},{2,34}... | collective-permute-start | bytes 3145736 | tf_op jit(solution)/shard_map/ppermute | solution.py:191
  34.6 33.9 %collective-permute-start.1 = (f32[32,8,1024]{2,1,0:T(8,128)S(1)}, f32[32,8,1024]{2,1,0:T(8,128)}, u32[]{:S(2)}, u32[]{:S(2)}) collective-permute-start(f32[32,8,1024]{2,1,0:T(8,128)S(1)} %all_to_all.50.refs_0_), channel_id=1, source_target_pairs={{0,96},{32,0},{64,32},{96,64},{1,97},{33,1},{65,33},{97,65},{2,98}... | collective-permute-start | bytes 3145736 | tf_op jit(solution)/shard_map/ppermute | solution.py:191
  36.9 29.5 %copy-start.10 = (s32[8]{0:T(128)S(1)}, s32[8]{0:T(128)}, u32[]{:S(2)}) copy-start(s32[8]{0:T(128)} %param.10) | copy-start | bytes 100
  53.1 29.5 %copy-start.4 = (f32[32,8,1024]{2,1,0:T(8,128)}, f32[32,8,1024]{2,1,0:T(8,128)S(1)}, u32[]{:S(2)}) copy-start(f32[32,8,1024]{2,1,0:T(8,128)S(1)} %all-to-all-done.1.refs_0_) | copy-start | bytes 3145732
  55.7 24.2 %all-to-all-start.2 = ((f32[32,8,1024]{2,1,0:T(8,128)}), f32[32,8,1024]{2,1,0:T(8,128)S(1)}, u32[]{:S(2)}, u32[]{:S(2)}) async-start(f32[32,8,1024]{2,1,0:T(8,128)} %bitcast.7), calls=%async_computation.2 | async-start | bytes 2097152 | tf_op jit(solution)/shard_map/all_to_all | solution.py:187
  63.1 39.0 %collective-permute-start.4 = (f32[32,8,1024]{2,1,0:T(8,128)S(1)}, f32[32,8,1024]{2,1,0:T(8,128)}, u32[]{:S(2)}, u32[]{:S(2)}) collective-permute-start(f32[32,8,1024]{2,1,0:T(8,128)S(1)} %all-to-all-done.1.refs_0_), channel_id=1, source_target_pairs={{0,32},{32,64},{64,96},{96,0},{1,33},{33,65},{65,97},{97,1},{2,34}... | collective-permute-start | bytes 3145736 | tf_op jit(solution)/shard_map/ppermute | solution.py:191
  63.4 39.4 %collective-permute-start.5 = (f32[32,8,1024]{2,1,0:T(8,128)S(1)}, f32[32,8,1024]{2,1,0:T(8,128)}, u32[]{:S(2)}, u32[]{:S(2)}) collective-permute-start(f32[32,8,1024]{2,1,0:T(8,128)S(1)} %all-to-all-done.1.refs_0_), channel_id=1, source_target_pairs={{0,96},{32,0},{64,32},{96,64},{1,97},{33,1},{65,33},{97,65},{2,98}... | collective-permute-start | bytes 3145736 | tf_op jit(solution)/shard_map/ppermute | solution.py:191
  68.5 33.2 %collective-permute-start.2 = (f32[16,8,1024]{2,1,0:T(8,128)}, f32[16,8,1024]{2,1,0:T(8,128)}, u32[]{:S(2)}, u32[]{:S(2)}) collective-permute-start(f32[16,8,1024]{2,1,0:T(8,128)} %slice.60), channel_id=1, source_target_pairs={{0,32},{32,64},{64,96},{96,0},{1,33},{33,65},{65,97},{97,1},{2,34}... | collective-permute-start | bytes 1572872 | tf_op jit(solution)/shard_map/ppermute | solution.py:191
  69.6 32.5 %collective-permute-start.3 = (f32[16,8,1024]{2,1,0:T(8,128)S(1)}, f32[16,8,1024]{2,1,0:T(8,128)S(1)}, u32[]{:S(2)}, u32[]{:S(2)}) collective-permute-start(f32[16,8,1024]{2,1,0:T(8,128)S(1)} %slice.61), channel_id=1, source_target_pairs={{0,96},{32,0},{64,32},{96,64},{1,97},{33,1},{65,33},{97,65},{2,98}... | collective-permute-start | bytes 1572872 | tf_op jit(solution)/shard_map/ppermute | solution.py:191
  79.9 42.0 %copy-start.3 = (f32[32,8,1024]{2,1,0:T(8,128)}, f32[32,8,1024]{2,1,0:T(8,128)S(1)}, u32[]{:S(2)}) copy-start(f32[32,8,1024]{2,1,0:T(8,128)S(1)} %all-to-all-done.2.refs_0_) | copy-start | bytes 3145732
  82.6 39.5 %all-to-all-start.4 = ((f32[32,8,1024]{2,1,0:T(8,128)}), f32[32,8,1024]{2,1,0:T(8,128)}, u32[]{:S(2)}, u32[]{:S(2)}) async-start(f32[32,8,1024]{2,1,0:T(8,128)} %bitcast.10), calls=%async_computation.4 | async-start | bytes 2097152 | tf_op jit(solution)/shard_map/all_to_all | solution.py:187
  88.4 50.0 %collective-permute-start.9 = (f32[32,8,1024]{2,1,0:T(8,128)S(1)}, f32[32,8,1024]{2,1,0:T(8,128)}, u32[]{:S(2)}, u32[]{:S(2)}) collective-permute-start(f32[32,8,1024]{2,1,0:T(8,128)S(1)} %all-to-all-done.2.refs_0_), channel_id=1, source_target_pairs={{0,32},{32,64},{64,96},{96,0},{1,33},{33,65},{65,97},{97,1},{2,34}... | collective-permute-start | bytes 3145736 | tf_op jit(solution)/shard_map/ppermute | solution.py:191
  101.7 36.8 %collective-permute-start.10 = (f32[32,8,1024]{2,1,0:T(8,128)S(1)}, f32[32,8,1024]{2,1,0:T(8,128)}, u32[]{:S(2)}, u32[]{:S(2)}) collective-permute-start(f32[32,8,1024]{2,1,0:T(8,128)S(1)} %all-to-all-done.2.refs_0_), channel_id=1, source_target_pairs={{0,96},{32,0},{64,32},{96,64},{1,97},{33,1},{65,33},{97,65},{2,98}... | collective-permute-start | bytes 3145736 | tf_op jit(solution)/shard_map/ppermute | solution.py:191
  102.0 0.8 copy-start.9
  103.9 30.8 %collective-permute-start.7 = (f32[16,8,1024]{2,1,0:T(8,128)S(1)}, f32[16,8,1024]{2,1,0:T(8,128)}, u32[]{:S(2)}, u32[]{:S(2)}) collective-permute-start(f32[16,8,1024]{2,1,0:T(8,128)S(1)} %slice.62), channel_id=1, source_target_pairs={{0,32},{32,64},{64,96},{96,0},{1,33},{33,65},{65,97},{97,1},{2,34}... | collective-permute-start | bytes 1572872 | tf_op jit(solution)/shard_map/ppermute | solution.py:191
  106.8 30.2 %collective-permute-start.8 = (f32[16,8,1024]{2,1,0:T(8,128)S(1)}, f32[16,8,1024]{2,1,0:T(8,128)}, u32[]{:S(2)}, u32[]{:S(2)}) collective-permute-start(f32[16,8,1024]{2,1,0:T(8,128)S(1)} %slice.63), channel_id=1, source_target_pairs={{0,96},{32,0},{64,32},{96,64},{1,97},{33,1},{65,33},{97,65},{2,98}... | collective-permute-start | bytes 1572872 | tf_op jit(solution)/shard_map/ppermute | solution.py:191
  121.9 37.2 %collective-permute-start.6 = (f32[16,4,1,8,512]{4,3,2,1,0:T(8,128)}, f32[16,4,1,8,512]{4,3,2,1,0:T(8,128)S(1)}, u32[]{:S(2)}, u32[]{:S(2)}) collective-permute-start(f32[16,4,1,8,512]{4,3,2,1,0:T(8,128)} %get-tuple-element.57), channel_id=1, source_target_pairs={{0,1},{1,0},{2,3},{3,2},{4,5},{5,4},{6,7},{7,6},{8,9},{9,8},{10,11... | collective-permute-start | bytes 3145736 | tf_op jit(solution)/shard_map/ppermute | solution.py:238
  124.3 36.1 %all-to-all-start.6 = ((f32[32,8,1024]{2,1,0:T(8,128)}), f32[32,8,1024]{2,1,0:T(8,128)}, u32[]{:S(2)}, u32[]{:S(2)}) async-start(f32[32,8,1024]{2,1,0:T(8,128)} %bitcast.13), calls=%async_computation.6 | async-start | bytes 2097152 | tf_op jit(solution)/shard_map/all_to_all | solution.py:187
  134.8 40.5 %collective-permute-start.14 = (f32[32,8,1024]{2,1,0:T(8,128)}, f32[32,8,1024]{2,1,0:T(8,128)}, u32[]{:S(2)}, u32[]{:S(2)}) collective-permute-start(f32[32,8,1024]{2,1,0:T(8,128)} %all-to-all-done.4.refs_0_), channel_id=1, source_target_pairs={{0,32},{32,64},{64,96},{96,0},{1,33},{33,65},{65,97},{97,1},{2,34}... | collective-permute-start | bytes 3145736 | tf_op jit(solution)/shard_map/ppermute | solution.py:191
  136.9 38.4 %collective-permute-start.15 = (f32[32,8,1024]{2,1,0:T(8,128)}, f32[32,8,1024]{2,1,0:T(8,128)}, u32[]{:S(2)}, u32[]{:S(2)}) collective-permute-start(f32[32,8,1024]{2,1,0:T(8,128)} %all-to-all-done.4.refs_0_), channel_id=1, source_target_pairs={{0,96},{32,0},{64,32},{96,64},{1,97},{33,1},{65,33},{97,65},{2,98}... | collective-permute-start | bytes 3145736 | tf_op jit(solution)/shard_map/ppermute | solution.py:191
  140.4 31.7 %collective-permute-start.12 = (f32[16,8,1024]{2,1,0:T(8,128)}, f32[16,8,1024]{2,1,0:T(8,128)}, u32[]{:S(2)}, u32[]{:S(2)}) collective-permute-start(f32[16,8,1024]{2,1,0:T(8,128)} %slice.64), channel_id=1, source_target_pairs={{0,32},{32,64},{64,96},{96,0},{1,33},{33,65},{65,97},{97,1},{2,34}... | collective-permute-start | bytes 1572872 | tf_op jit(solution)/shard_map/ppermute | solution.py:191
  142.7 29.3 %collective-permute-start.13 = (f32[16,8,1024]{2,1,0:T(8,128)}, f32[16,8,1024]{2,1,0:T(8,128)}, u32[]{:S(2)}, u32[]{:S(2)}) collective-permute-start(f32[16,8,1024]{2,1,0:T(8,128)} %slice.65), channel_id=1, source_target_pairs={{0,96},{32,0},{64,32},{96,64},{1,97},{33,1},{65,33},{97,65},{2,98}... | collective-permute-start | bytes 1572872 | tf_op jit(solution)/shard_map/ppermute | solution.py:191
  145.5 13.7 %copy-start.2 = (f32[16,4,1,8,512]{4,3,2,1,0:T(8,128)S(1)}, f32[16,4,1,8,512]{4,3,2,1,0:T(8,128)}, u32[]{:S(2)}) copy-start(f32[16,4,1,8,512]{4,3,2,1,0:T(8,128)} %get-tuple-element.56) | copy-start | bytes 3145732
  159.1 36.9 %collective-permute-start.11 = (f32[16,4,1,8,512]{4,3,2,1,0:T(8,128)}, f32[16,4,1,8,512]{4,3,2,1,0:T(8,128)S(1)}, u32[]{:S(2)}, u32[]{:S(2)}) collective-permute-start(f32[16,4,1,8,512]{4,3,2,1,0:T(8,128)} %get-tuple-element.65), channel_id=1, source_target_pairs={{0,1},{1,0},{2,3},{3,2},{4,5},{5,4},{6,7},{7,6},{8,9},{9,8},{10,11... | collective-permute-start | bytes 3145736 | tf_op jit(solution)/shard_map/ppermute | solution.py:238
  160.4 36.9 %all-to-all-start.3 = ((f32[16,4,1,8,512]{4,3,2,1,0:T(8,128)}), f32[16,4,1,8,512]{4,3,2,1,0:T(8,128)S(1)}, u32[]{:S(2)}, u32[]{:S(2)}) async-start(f32[16,4,1,8,512]{4,3,2,1,0:T(8,128)} %add.83), calls=%async_computation.3 | async-start | bytes 2097152 | tf_op jit(solution)/shard_map/all_to_all | solution.py:242
  172.1 36.4 %collective-permute-start.19 = (f32[32,8,1024]{2,1,0:T(8,128)}, f32[32,8,1024]{2,1,0:T(8,128)}, u32[]{:S(2)}, u32[]{:S(2)}) collective-permute-start(f32[32,8,1024]{2,1,0:T(8,128)} %all-to-all-done.6.refs_0_), channel_id=1, source_target_pairs={{0,32},{32,64},{64,96},{96,0},{1,33},{33,65},{65,97},{97,1},{2,34}... | collective-permute-start | bytes 3145736 | tf_op jit(solution)/shard_map/ppermute | solution.py:191
  172.1 36.4 %collective-permute-start.20 = (f32[32,8,1024]{2,1,0:T(8,128)}, f32[32,8,1024]{2,1,0:T(8,128)}, u32[]{:S(2)}, u32[]{:S(2)}) collective-permute-start(f32[32,8,1024]{2,1,0:T(8,128)} %all-to-all-done.6.refs_0_), channel_id=1, source_target_pairs={{0,96},{32,0},{64,32},{96,64},{1,97},{33,1},{65,33},{97,65},{2,98}... | collective-permute-start | bytes 3145736 | tf_op jit(solution)/shard_map/ppermute | solution.py:191
  177.2 31.2 %collective-permute-start.17 = (f32[16,8,1024]{2,1,0:T(8,128)}, f32[16,8,1024]{2,1,0:T(8,128)}, u32[]{:S(2)}, u32[]{:S(2)}) collective-permute-start(f32[16,8,1024]{2,1,0:T(8,128)} %slice.66), channel_id=1, source_target_pairs={{0,32},{32,64},{64,96},{96,0},{1,33},{33,65},{65,97},{97,1},{2,34}... | collective-permute-start | bytes 1572872 | tf_op jit(solution)/shard_map/ppermute | solution.py:191
  179.1 29.3 %collective-permute-start.18 = (f32[16,8,1024]{2,1,0:T(8,128)}, f32[16,8,1024]{2,1,0:T(8,128)}, u32[]{:S(2)}, u32[]{:S(2)}) collective-permute-start(f32[16,8,1024]{2,1,0:T(8,128)} %slice.67), channel_id=1, source_target_pairs={{0,96},{32,0},{64,32},{96,64},{1,97},{33,1},{65,33},{97,65},{2,98}... | collective-permute-start | bytes 1572872 | tf_op jit(solution)/shard_map/ppermute | solution.py:191
  182.3 13.8 %copy-start.1 = (f32[16,4,1,8,512]{4,3,2,1,0:T(8,128)S(1)}, f32[16,4,1,8,512]{4,3,2,1,0:T(8,128)}, u32[]{:S(2)}) copy-start(f32[16,4,1,8,512]{4,3,2,1,0:T(8,128)} %get-tuple-element.64) | copy-start | bytes 3145732
  196.0 32.7 %collective-permute-start.16 = (f32[16,4,1,8,512]{4,3,2,1,0:T(8,128)}, f32[16,4,1,8,512]{4,3,2,1,0:T(8,128)}, u32[]{:S(2)}, u32[]{:S(2)}) collective-permute-start(f32[16,4,1,8,512]{4,3,2,1,0:T(8,128)} %get-tuple-element.73), channel_id=1, source_target_pairs={{0,1},{1,0},{2,3},{3,2},{4,5},{5,4},{6,7},{7,6},{8,9},{9,8},{10,11... | collective-permute-start | bytes 3145736 | tf_op jit(solution)/shard_map/ppermute | solution.py:238
  197.3 33.8 %all-to-all-start.5 = ((f32[16,4,1,8,512]{4,3,2,1,0:T(8,128)}), f32[16,4,1,8,512]{4,3,2,1,0:T(8,128)S(1)}, u32[]{:S(2)}, u32[]{:S(2)}) async-start(f32[16,4,1,8,512]{4,3,2,1,0:T(8,128)} %add.85), calls=%async_computation.5 | async-start | bytes 2097152 | tf_op jit(solution)/shard_map/all_to_all | solution.py:242
  209.5 19.1 %collective-permute-start.21 = (f32[16,8,1024]{2,1,0:T(8,128)S(1)}, f32[16,8,1024]{2,1,0:T(8,128)}, u32[]{:S(2)}, u32[]{:S(2)}) collective-permute-start(f32[16,8,1024]{2,1,0:T(8,128)S(1)} %slice.68), channel_id=1, source_target_pairs={{0,32},{32,64},{64,96},{96,0},{1,33},{33,65},{65,97},{97,1},{2,34}... | collective-permute-start | bytes 1572872 | tf_op jit(solution)/shard_map/ppermute | solution.py:191
  211.7 16.9 %collective-permute-start.22 = (f32[16,8,1024]{2,1,0:T(8,128)}, f32[16,8,1024]{2,1,0:T(8,128)}, u32[]{:S(2)}, u32[]{:S(2)}) collective-permute-start(f32[16,8,1024]{2,1,0:T(8,128)} %slice.69), channel_id=1, source_target_pairs={{0,96},{32,0},{64,32},{96,64},{1,97},{33,1},{65,33},{97,65},{2,98}... | collective-permute-start | bytes 1572872 | tf_op jit(solution)/shard_map/ppermute | solution.py:191
  214.9 13.8 %copy-start = (f32[16,4,1,8,512]{4,3,2,1,0:T(8,128)S(1)}, f32[16,4,1,8,512]{4,3,2,1,0:T(8,128)}, u32[]{:S(2)}) copy-start(f32[16,4,1,8,512]{4,3,2,1,0:T(8,128)} %get-tuple-element.72) | copy-start | bytes 3145732
  228.6 23.0 %collective-permute-start.23 = (f32[16,4,1,8,512]{4,3,2,1,0:T(8,128)}, f32[16,4,1,8,512]{4,3,2,1,0:T(8,128)}, u32[]{:S(2)}, u32[]{:S(2)}) collective-permute-start(f32[16,4,1,8,512]{4,3,2,1,0:T(8,128)} %get-tuple-element.81), channel_id=1, source_target_pairs={{0,1},{1,0},{2,3},{3,2},{4,5},{5,4},{6,7},{7,6},{8,9},{9,8},{10,11... | collective-permute-start | bytes 3145736 | tf_op jit(solution)/shard_map/ppermute | solution.py:238
  231.1 25.1 %all-to-all-start.7 = ((f32[16,4,1,8,512]{4,3,2,1,0:T(8,128)}), f32[16,4,1,8,512]{4,3,2,1,0:T(8,128)S(1)}, u32[]{:S(2)}, u32[]{:S(2)}) async-start(f32[16,4,1,8,512]{4,3,2,1,0:T(8,128)} %add.87), calls=%async_computation.7 | async-start | bytes 2097152 | tf_op jit(solution)/shard_map/all_to_all | solution.py:242
  251.3 10.5 %copy-start.6 = (f32[8,512]{1,0:T(8,128)S(1)}, f32[8,512]{1,0:T(8,128)}, u32[]{:S(2)}) copy-start(f32[8,512]{1,0:T(8,128)} %param.9) | copy-start | bytes 49156
  251.3 11.4 %collective-permute-start.24 = (f32[16,4,1,8,512]{4,3,2,1,0:T(8,128)}, f32[16,4,1,8,512]{4,3,2,1,0:T(8,128)}, u32[]{:S(2)}, u32[]{:S(2)}) collective-permute-start(f32[16,4,1,8,512]{4,3,2,1,0:T(8,128)} %get-tuple-element.88), channel_id=1, source_target_pairs={{0,1},{1,0},{2,3},{3,2},{4,5},{5,4},{6,7},{7,6},{8,9},{9,8},{10,11... | collective-permute-start | bytes 3145736 | tf_op jit(solution)/shard_map/ppermute | solution.py:238
  256.2 23.8 %all-to-all-start.8 = ((f32[16,4,1,8,512]{4,3,2,1,0:T(8,128)}), f32[16,4,1,8,512]{4,3,2,1,0:T(8,128)}, u32[]{:S(2)}, u32[]{:S(2)}) async-start(f32[16,4,1,8,512]{4,3,2,1,0:T(8,128)} %add.89), calls=%async_computation.8 | async-start | bytes 2097152 | tf_op jit(solution)/shard_map/all_to_all | solution.py:242
  262.7 39.2 %copy-start.7 = (f32[160]{0:T(256)S(1)}, f32[160]{0:T(256)}, u32[]{:S(2)}) copy-start(f32[160]{0:T(256)} %param.8) | copy-start | bytes 1924
  280.0 20.6 %all-to-all-start.9 = ((f32[16,4,1,8,512]{4,3,2,1,0:T(8,128)}), f32[16,4,1,8,512]{4,3,2,1,0:T(8,128)}, u32[]{:S(2)}, u32[]{:S(2)}) async-start(f32[16,4,1,8,512]{4,3,2,1,0:T(8,128)} %add.91), calls=%async_computation.9 | async-start | bytes 2097152 | tf_op jit(solution)/shard_map/all_to_all | solution.py:242
